TPU v7x, 512 devices: a whole 4x8x8 slice. The times are simulated.
512 devices in a mesh: section: 8 (over y_hi, x), ctx: 64 (over y_lo, z, core).
Axes of the slice: x: 4, y: 8 (y_hi: 2, y_lo: 4; y = y_hi * 4 + y_lo), z: 8, core: 2. Of those that a mesh axis runs over, the one named last changes fastest.
Arguments:
- inputs: bfloat16 [8192, 2048], P('ctx', 'section'), may hold values from -8 to 8
- out_grads: bfloat16 [8192, 2048], P('ctx', 'section'), may hold values from -6 to 6
- conv_weight: float32 [3, 4, 2048], P(None, None, 'section'), may hold values from -3 to 3
- log_decay: float32 [8192, 2048], P('ctx', 'section'), may hold values from -1 to 0
- beta: float32 [8192, 16], P('ctx', 'section'), may hold values from 0 to 1
Outputs:
- stream_out: bfloat16 [8192, 2048], P('ctx', 'section')
- input_grad: bfloat16 [8192, 2048], P('ctx', 'section')
All inputs are finite; a program needn't handle non-finite values.
Results may differ from a plain program's by a relative error of at most 0.001.
Values sent between devices are 32-bit elements; how exact they have to be, the bound alone decides.
A program may use at most 128 MiB of HBM per device.

v0:
```python
import jax
import jax.numpy as jnp
from jax import lax
from jax.sharding import PartitionSpec as P

HEAD_DIM = 128


epsilon = 1e-06
norm_eps = 1e-05
highest = lax.Precision.HIGHEST


def passed_along(block, axis, distance):
    devices = range(lax.axis_size(axis))
    route = [(i - distance, i) for i in devices if i - distance in devices]
    return lax.ppermute(block, axis, route)


def entering(part, axis, combine, identity, reverse):
    count = lax.axis_size(axis)
    place = lax.axis_index(axis)
    ahead = count - 1 - place if reverse else place
    gathered = jax.tree.map(lambda a: lax.all_gather(a, axis), part)
    state = jax.tree.map(lambda a, e: jnp.zeros_like(a) + jnp.asarray(e, a.dtype), part, identity)

    def one(hop, state):
        source = count - 1 - hop if reverse else hop
        return combine(
            state, jax.tree.map(lambda a: lax.dynamic_index_in_dim(a, source, 0, False), gathered)
        )

    return lax.fori_loop(0, ahead, one, state)


def unit_rows(mixed):
    act = jax.nn.silu(mixed).reshape(mixed.shape[0], -1, HEAD_DIM)
    return act / jnp.sqrt(jnp.sum(act * act, axis=-1, keepdims=True) + epsilon)


def features(padded, kern):
    taps_count = kern.shape[1]
    length = padded.shape[0] - taps_count + 1
    mixes = [
        sum((kern[j, i] * padded[i : i + length] for i in range(taps_count))) for j in range(3)
    ]
    queries = unit_rows(mixes[0])
    keys = unit_rows(mixes[1])
    values = jax.nn.silu(mixes[2]).reshape(length, -1, HEAD_DIM)
    return (queries, keys, values)


def solve_block(keys, values, cumulative, rates):
    length = keys.shape[0]
    middle = cumulative[length // 2]
    key_fwd = keys * jnp.exp(cumulative - middle)
    key_back = keys * jnp.exp(middle - cumulative)
    products = jnp.einsum("thc,shc->hts", key_fwd, key_back, precision=highest)
    strict_mask = jnp.tril(jnp.ones((length, length), jnp.float32), -1)
    rate_col = jnp.swapaxes(rates, 0, 1)[:, :, None]
    system = jnp.eye(length, dtype=jnp.float32) + rate_col * products * strict_mask
    rhs_keys = rate_col * jnp.swapaxes(keys * jnp.exp(cumulative), 0, 1)
    rhs_values = rate_col * jnp.swapaxes(values, 0, 1)
    solved = lax.linalg.triangular_solve(
        system,
        jnp.concatenate([rhs_keys, rhs_values], axis=-1),
        left_side=True,
        lower=True,
        unit_diagonal=True,
    )
    return (solved[..., :HEAD_DIM], solved[..., HEAD_DIM:])


def transition(keys, cumulative, w_rows, u_rows):
    final_decay = cumulative[-1]
    key_end = keys * jnp.exp(final_decay - cumulative)
    retained = jnp.exp(final_decay)[:, :, None] * jnp.eye(HEAD_DIM, dtype=jnp.float32)
    transit = retained - jnp.einsum("thd,hte->hde", key_end, w_rows, precision=highest)
    inject = jnp.einsum("thd,hte->hde", key_end, u_rows, precision=highest)
    return (transit, inject)


def block_out(queries, keys, cumulative, w_rows, u_rows, start):
    length = queries.shape[0]
    middle = cumulative[length // 2]
    query_fwd = queries * jnp.exp(cumulative - middle)
    key_back = keys * jnp.exp(middle - cumulative)
    full_mask = jnp.tril(jnp.ones((length, length), jnp.float32))
    scores = jnp.einsum("thc,shc->hts", query_fwd, key_back, precision=highest) * full_mask
    fresh = u_rows - jnp.einsum("htd,hde->hte", w_rows, start, precision=highest)
    output = jnp.einsum("thd,hde->the", queries * jnp.exp(cumulative), start, precision=highest)
    output = output + jnp.einsum("hts,hse->the", scores, fresh, precision=highest)
    return output.reshape(length, -1)


def compose(earlier, later):
    first_map, first_add = earlier
    second_map, second_add = later
    joined_map = jnp.einsum("hab,hbc->hac", second_map, first_map, precision=highest)
    joined_add = jnp.einsum("hab,hbc->hac", second_map, first_add, precision=highest) + second_add
    return (joined_map, joined_add)


def unit_pair(elements):
    return (
        jnp.broadcast_to(jnp.eye(HEAD_DIM, dtype=jnp.float32), elements[0].shape),
        jnp.zeros_like(elements[1]),
    )


def pass_rim(piece, offset):
    return passed_along(piece, "ctx", offset)


def section_sum(values):
    return lax.psum(values, "section")


def shards(inputs, out_grads, conv_weight, log_decay, beta):
    length, channels = inputs.shape
    tail = conv_weight.shape[1] - 1
    width_all = channels * lax.axis_size("section")
    cumulative = jnp.cumsum(log_decay.reshape(length, -1, HEAD_DIM), axis=0)
    stream = inputs.astype(jnp.float32)
    scale = 1.0 / jnp.sqrt(section_sum(jnp.sum(stream * stream, axis=1)) / width_all + norm_eps)
    normed = stream * scale[:, None]
    rim = pass_rim(normed[length - tail :], 1)

    def front(stream_part, rim_part):
        return features(jnp.concatenate([rim_part, stream_part], axis=0), conv_weight)

    queries, keys, values = front(normed, rim)
    w_rows, u_rows = solve_block(keys, values, cumulative, beta)
    transit, inject = transition(keys, cumulative, w_rows, u_rows)
    start = entering((transit, inject), "ctx", compose, unit_pair((transit, inject)), False)[1]
    output = (stream + block_out(queries, keys, cumulative, w_rows, u_rows, start)).astype(
        jnp.bfloat16
    )
    _, pull_front = jax.vjp(front, normed, rim)
    _, pull_solve = jax.vjp(
        lambda key_x, value_x: solve_block(key_x, value_x, cumulative, beta), keys, values
    )
    _, pull_trans = jax.vjp(
        lambda key_x, w_x, u_x: transition(key_x, cumulative, w_x, u_x), keys, w_rows, u_rows
    )
    grad_out = out_grads.astype(jnp.float32)
    _, pull_out = jax.vjp(
        lambda q_x, k_x, w_x, u_x, s_x: block_out(q_x, k_x, cumulative, w_x, u_x, s_x),
        queries,
        keys,
        w_rows,
        u_rows,
        start,
    )
    grad_query, grad_key_out, grad_w_out, grad_u_out, grad_start = pull_out(grad_out)
    back_elements = (jnp.swapaxes(transit, 1, 2), grad_start)
    _, grad_end = entering(back_elements, "ctx", compose, unit_pair(back_elements), True)
    grad_transit = jnp.einsum("hde,hfe->hdf", grad_end, start, precision=highest)
    grad_key_trans, grad_w_trans, grad_u_trans = pull_trans((grad_transit, grad_end))
    grad_key_solve, grad_value = pull_solve((grad_w_out + grad_w_trans, grad_u_out + grad_u_trans))
    grad_normed, grad_rim = pull_front(
        (grad_query, grad_key_out + grad_key_trans + grad_key_solve, grad_value)
    )
    from_next = pass_rim(grad_rim, -1)
    grad_normed = jnp.concatenate(
        [grad_normed[: length - tail], grad_normed[length - tail :] + from_next], axis=0
    )
    inner = section_sum(jnp.sum(grad_normed * stream, axis=1))
    cubed = scale * scale * scale
    total = grad_out + grad_normed * scale[:, None] - stream * (cubed * inner / width_all)[:, None]
    return (output, total.astype(jnp.bfloat16))


def solution(mesh):
    in_specs = (
        P("ctx", "section"),
        P("ctx", "section"),
        P(None, None, "section"),
        P("ctx", "section"),
        P("ctx", "section"),
    )
    out_specs = (P("ctx", "section"), P("ctx", "section"))
    return jax.shard_map(shards, mesh=mesh, in_specs=in_specs, out_specs=out_specs, check_vma=False)
```

profile of v0, /device:TPU:1, one launch (start us, length us, event | category | flops | bytes accessed | tf_op | source)
XLA Modules:
  0.0 698.3 jit_solution(6151853313327553937)
XLA Ops:
  8.2 28.8 %psum.14 = f32[128]{0:T(128)S(1)} all-reduce(f32[128]{0:T(128)S(1)} %fusion.39), channel_id=1, replica_groups=mesh['section'=8,'ctx'=64] {'section'}, use_global_device_ids=true, to_apply=%region_2.3 | all-reduce | flops 128 | bytes 1024 | tf_op jit(solution)/shard_map/psum | solution.py:116
  37.2 8.3 %collective-permute-start = (f32[3,256]{0,1:T(8,128)S(1)}, f32[3,256]{0,1:T(8,128)S(1)}, u32[]{:S(2)}, u32[]{:S(2)}) collective-permute-start(f32[3,256]{0,1:T(8,128)S(1)} %slice.132), channel_id=1, source_target_pairs={{0,1},{1,2},{2,3},{3,4},{4,5},{5,6},{6,7},{7,8},{8,9},{9,10},{10,1... | collective-permute-start | bytes 9224 | tf_op jit(solution)/shard_map/ppermute | solution.py:17
  49.7 19.7 %custom-call.9 = f32[2,1,128,128]{2,3,1,0:T(8,128)S(1)} custom-call(f32[2,1,128,128]{3,2,1,0:T(8,128)S(1)} %fusion.26), custom_call_target="InvertDiagBlocksLowerTriangular" | custom-call | tf_op jit(solution)/shard_map/triangular_solve/custom-call.1 | solution.py:64
  74.7 119.5 %all-gather.11.cloned.1.call-done = f32[128,128,128]{2,1,0:T(8,128)} async-done(((f32[2,128,128]{2,1,0:T(8,128)}), f32[128,128,128]{2,1,0:T(8,128)}) %all-gather.11.cloned.1.call-update) | async-done | bytes 8388624 | tf_op jit(solution)/shard_map/all_gather | solution.py:24
  194.3 125.1 %all-gather.9.cloned.1.call-done = f32[128,128,128]{2,1,0:T(8,128)} async-done(((f32[2,128,128]{2,1,0:T(8,128)}), f32[128,128,128]{2,1,0:T(8,128)}) %all-gather.9.cloned.1.call-update) | async-done | bytes 8388624 | tf_op jit(solution)/shard_map/all_gather | solution.py:24
  319.4 1.3 while.26
  325.3 119.1 %all-gather.13.cloned.1.call-done = f32[128,128,128]{2,1,0:T(8,128)} async-done(((f32[2,128,128]{2,1,0:T(8,128)}), f32[128,128,128]{2,1,0:T(8,128)}) %all-gather.13.cloned.1.call-update) | async-done | bytes 8388624 | tf_op jit(solution)/shard_map/all_gather | solution.py:24
  444.4 124.9 %all-gather.15.cloned.1.call-done = f32[128,128,128]{2,1,0:T(8,128)} async-done(((f32[2,128,128]{2,1,0:T(8,128)}), f32[128,128,128]{2,1,0:T(8,128)}) %all-gather.15.cloned.1.call-update) | async-done | bytes 8388624 | tf_op jit(solution)/shard_map/all_gather | solution.py:24
  569.4 80.3 %while.27 = (s32[]{:T(128)}, f32[2,128,128]{2,1,0:T(8,128)S(1)}, s32[]{:T(128)}, f32[64,2,128,128]{3,2,1,0:T(8,128)}, f32[64,2,128,128]{3,2,1,0:T(8,128)}, /*index=5*/s32[]{:T(128)}, s32[]{:T(128)}, s32[]{:T(128)}, s32[]{:T(128)}) while((s32[]{:T(128)}, f32[2,128,128]{2,1,0:T(8,128)S(1)}, s32[]{:T(128)}, f32[64,2,128,128]{3,2,1,0:T(8,128)}, ...), condition=%wide.region_8.10_spmd, body=%wide.region_7.9_spmd.sunk | while | flops 50364420 | bytes 787595 | solution.py:33
  569.4 1.2 convolution_add_fusion.10
  570.7 1.2 convolution_add_fusion.10
  572.0 1.2 convolution_add_fusion.10
  573.3 1.2 convolution_add_fusion.10
  574.6 1.2 convolution_add_fusion.10
  577.2 1.2 convolution_add_fusion.10
  578.5 1.2 convolution_add_fusion.10
  579.8 1.2 convolution_add_fusion.10
  581.1 1.2 convolution_add_fusion.10
  582.4 1.2 convolution_add_fusion.10
  583.7 1.2 convolution_add_fusion.10
  584.9 1.2 convolution_add_fusion.10
  586.2 1.2 convolution_add_fusion.10
  588.8 1.2 convolution_add_fusion.10
  590.1 1.2 convolution_add_fusion.10
  591.4 1.2 convolution_add_fusion.10
  592.7 1.2 convolution_add_fusion.10
  595.3 1.2 convolution_add_fusion.10
  596.6 1.2 convolution_add_fusion.10
  597.9 1.2 convolution_add_fusion.10
  599.2 1.2 convolution_add_fusion.10
  600.4 1.2 convolution_add_fusion.10
  601.7 1.2 convolution_add_fusion.10
  603.0 1.2 convolution_add_fusion.10
  604.3 1.2 convolution_add_fusion.10
  606.9 1.2 convolution_add_fusion.10
  608.2 1.2 convolution_add_fusion.10
  609.5 1.2 convolution_add_fusion.10
  610.8 1.2 convolution_add_fusion.10
  613.4 1.2 convolution_add_fusion.10
  614.7 1.2 convolution_add_fusion.10
  616.0 1.2 convolution_add_fusion.10
  617.2 1.2 convolution_add_fusion.10
  618.5 1.2 convolution_add_fusion.10
  619.8 1.2 convolution_add_fusion.10
  621.1 1.2 convolution_add_fusion.10
  622.4 1.2 convolution_add_fusion.10
  625.0 1.2 convolution_add_fusion.10
  626.3 1.2 convolution_add_fusion.10
  627.6 1.2 convolution_add_fusion.10
  628.9 1.2 convolution_add_fusion.10
  631.5 1.2 convolution_add_fusion.10
  632.7 1.2 convolution_add_fusion.10
  634.0 1.2 convolution_add_fusion.10
  635.3 1.2 convolution_add_fusion.10
  636.6 1.2 convolution_add_fusion.10
  637.9 1.2 convolution_add_fusion.10
  640.5 1.2 convolution_add_fusion.10
  643.1 1.2 convolution_add_fusion.10
  644.4 1.2 convolution_add_fusion.10
  645.7 1.2 convolution_add_fusion.10
  647.0 1.2 convolution_add_fusion.10
  655.8 3.5 collective-permute-start.1
  659.8 2.3 collective-permute-done.1
  662.2 28.0 %psum.15 = f32[128]{0:T(128)S(1)} all-reduce(f32[128]{0:T(128)S(1)} %fusion.41), channel_id=1, replica_groups=mesh['section'=8,'ctx'=64] {'section'}, use_global_device_ids=true, to_apply=%region_12.14 | all-reduce | flops 128 | bytes 1024 | tf_op jit(solution)/shard_map/psum | solution.py:116
  (166 shorter events, 37.5 us)
Async XLA Ops:
  7.2 67.3 %copy-start = (bf16[128,256]{1,0:T(8,128)(2,1)S(1)}, bf16[128,256]{1,0:T(8,128)(2,1)}, u32[]{:S(2)}) copy-start(bf16[128,256]{1,0:T(8,128)(2,1)} %param.12) | copy-start | bytes 196612
  7.2 187.1 %all-gather.11.cloned.1.call-start = ((), (), s32[]{:S(2)}) async-start(), calls=%async_computation.1 | async-start | bytes 8519680 | tf_op jit(solution)/shard_map/all_gather | solution.py:24
  37.2 10.6 %collective-permute-start = (f32[3,256]{0,1:T(8,128)S(1)}, f32[3,256]{0,1:T(8,128)S(1)}, u32[]{:S(2)}, u32[]{:S(2)}) collective-permute-start(f32[3,256]{0,1:T(8,128)S(1)} %slice.132), channel_id=1, source_target_pairs={{0,1},{1,2},{2,3},{3,4},{4,5},{5,6},{6,7},{7,8},{8,9},{9,10},{10,1... | collective-permute-start | bytes 9224 | tf_op jit(solution)/shard_map/ppermute | solution.py:17
  72.4 247.0 %all-gather.9.cloned.1.call-start = ((), (), s32[]{:S(2)}) async-start(), calls=%async_computation | async-start | bytes 8519680 | tf_op jit(solution)/shard_map/all_gather | solution.py:24
  73.5 371.0 %all-gather.13.cloned.1.call-start = ((), (), s32[]{:S(2)}) async-start(), calls=%async_computation.2 | async-start | bytes 8519680 | tf_op jit(solution)/shard_map/all_gather | solution.py:24
  74.4 495.0 %all-gather.15.cloned.1.call-start = ((), (), s32[]{:S(2)}) async-start(), calls=%async_computation.3 | async-start | bytes 8519680 | tf_op jit(solution)/shard_map/all_gather | solution.py:24
  319.4 332.4 %copy-start.1 = (f32[128,2]{0,1:T(2,128)S(1)}, f32[128,2]{0,1:T(2,128)}, u32[]{:S(2)}) copy-start(f32[128,2]{0,1:T(2,128)} %param.15) | copy-start | bytes 3076
  655.8 6.3 collective-permute-start.1
Sparse Core Ops, SparseCore 0:
  72.5 121.7 all-gather.10
  196.4 122.8 all-gather.8
  321.5 122.8 all-gather.12
  446.5 122.8 all-gather.14
where the time goes:
time: 700 us; the launch traced here: 698 us
  waiting for transfers between devices  491 us (70%)
  matrix products  90.6 us (13%)
  blocking collectives  56.8 us (8%)
  other arithmetic  24.2 us (3%)
  between operations  14.3 us (2%)
  starting transfers between devices  11.9 us (2%)
    all_gather x4, waiting for transfers between devices, entering(): gathered = jax.tree.map(lambda a: lax.all_gather(a, axis), part)  489 us
    dot_general x63, matrix products, compose(): jnp.einsum('hab,hbc->hac', second_map, first_add, precision=highest)  78.2 us
    psum x2, blocking collectives, section_sum(): return lax.psum(values, 'section')  56.8 us
    another operation x4, other arithmetic, solve_block(): lax.linalg.triangular_solve(system, jnp.concatenate([rhs_keys, rhs_values...  19.8 us
  transfers between devices with their start and end apart: 6, of which 5 were waited for; matrix products, arithmetic and copies ran while one was open for 2% of the time, Pallas kernels for 0%

commit v1 on v0

v1 whole, which is shorter than its diff:
```python
import functools

import jax
import jax.numpy as jnp
from jax import lax
from jax.experimental import pallas as pl
from jax.experimental.pallas import tpu as pltpu
from jax.sharding import PartitionSpec as P

MESH = pl.DeviceIdType.MESH
D = 128
F32 = jnp.float32
BF16 = jnp.bfloat16


def split2(a):
    high = a.astype(BF16)
    low = (a - high.astype(F32)).astype(BF16)
    return high, low


def raw_dot(a, b, ca, cb):
    return lax.dot_general(a, b, (((ca,), (cb,)), ((), ())), preferred_element_type=F32)


def mm(a, b, ca=1, cb=0):
    ah, al = split2(a)
    bh, bl = split2(b)
    return raw_dot(ah, bh, ca, cb) + (raw_dot(ah, bl, ca, cb) + raw_dot(al, bh, ca, cb))


def mm_nt(a, b):
    return mm(a, b, 1, 1)


def mm_tn(a, b):
    return mm(a, b, 0, 0)


def iota2(shape, axis):
    return lax.broadcasted_iota(jnp.int32, shape, axis)


def row_sums(values):
    high, low = split2(values)
    ones = jnp.ones((8, values.shape[1]), BF16)
    return raw_dot(ones, high, 1, 1) + raw_dot(ones, low, 1, 1)


def as_columns(tile):
    return jnp.transpose(jnp.broadcast_to(tile[0:1], (D, D)))


def unit_lower_inverse(strict_parts):
    r, c = iota2((D, D), 0), iota2((D, D), 1)
    eye = jnp.where(r == c, 1.0, 0.0).astype(F32)
    inverse = None
    for k in range(7):
        mask = ((r >> (k + 1)) == (c >> (k + 1))) & (((r >> k) & 1) == 1) & (((c >> k) & 1) == 0)
        off = [jnp.where(mask, a, 0.0) for a in strict_parts]
        if k == 0:
            inverse = [eye - o for o in off]
        else:
            half = [mm(m, o) for m, o in zip(inverse, off)]
            inverse = [m - mm(h, m) for h, m in zip(half, inverse)]
    return inverse


def kernel(geom, x_ref, do_ref, g_ref, beta_ref, w_ref, out_ref, dx_ref, *scratch):
    sections, n_y, n_z, width_all = geom
    (
        SB, XB, R, R2, TB, NP, RIM, RIMB, SC,
        QK, DS, EX, FB, WQ, UO, ZK, MAPS, TS, VS, VR, YB, SO, ST, DM, OB, OR, GB, GR,
        row_s, row_r, row2_s, row2_r, one_s, one_r, ring_s, ring_r, vec_s, vec_r, back_s, back_r,
    ) = scratch
    n_ctx = n_y * n_z * 2
    cols = D // n_z
    sec = lax.axis_index("section")
    ctx = lax.axis_index("ctx")
    core = lax.rem(ctx, 2)
    chip = ctx // 2
    y = chip // n_z
    z = lax.rem(chip, n_z)
    partner = ctx + 1 - 2 * core
    after = lax.rem(ctx + 2, n_ctx)
    before = lax.rem(ctx + n_ctx - 2, n_ctx)

    def at_z(zz):
        return y * (2 * n_z) + zz * 2 + core

    def at_y(yy):
        return yy * (2 * n_z) + z * 2 + core

    def copy_to(src, dst, ss, rs, to_sec, to_ctx):
        return pltpu.make_async_remote_copy(
            src_ref=src, dst_ref=dst, send_sem=ss, recv_sem=rs,
            device_id=(to_sec, to_ctx), device_id_type=MESH,
        )

    peers = [(ds, dc) for ds in range(sections) for dc in range(2) if ds or dc]

    barrier = pltpu.get_barrier_semaphore()

    def greet(to_sec, to_ctx):
        pl.semaphore_signal(barrier, inc=1, device_id=(to_sec, to_ctx), device_id_type=MESH)

    for ds, dc in peers:
        greet(lax.rem(sec + ds, sections), partner if dc else ctx)
    for dz in range(1, n_z):
        greet(sec, at_z(lax.rem(z + dz, n_z)))
    for dy in range(1, n_y):
        greet(sec, at_y(lax.rem(y + dy, n_y)))
    greet(sec, after)
    greet(sec, before)
    greeted = len(peers) + n_z - 1 + n_y - 1 + 2

    first = core == 0

    def halves(ref):
        whole = ref[...].astype(F32)
        low, high = whole[:, :D], whole[:, D:]
        return jnp.where(first, low, high), jnp.where(first, high, low), whole

    x_own, x_oth, x_all = halves(x_ref)
    d_own, d_oth, _ = halves(do_ref)
    g_own, g_oth, _ = halves(g_ref)
    b0 = jnp.broadcast_to(beta_ref[:, 0:1], (D, D))
    b1 = jnp.broadcast_to(beta_ref[:, 1:2], (D, D))
    SB[0] = x_oth
    SB[1] = d_oth
    SB[2] = g_oth
    SB[3] = jnp.where(first, b1, b0)
    XB[core, 0] = x_own
    XB[core, 1] = d_own
    XB[core, 2] = g_own
    XB[core, 3] = jnp.where(first, b0, b1)
    R[0] = row_sums(x_all * x_all)
    pl.semaphore_wait(barrier, greeted)

    row_copies = []
    for ds, dc in peers:
        back = ((sections - ds) % sections) * 2 + dc
        copy = copy_to(R.at[0], R.at[back], row_s.at[ds * 2 + dc], row_r.at[back],
                       lax.rem(sec + ds, sections), partner if dc else ctx)
        copy.start()
        row_copies.append(copy)
    swap = copy_to(SB, XB.at[core], one_s.at[0], one_r.at[0], sec, partner)
    swap.start()

    def rows_wait(buf, ss, rs):
        for ds, dc in peers:
            slot = ds * 2 + dc
            copy_to(buf.at[slot], buf.at[slot], ss.at[slot], rs.at[slot], sec, ctx).wait_recv()

    rows_wait(R, row_s, row_r)
    same = R[0]
    other = R[1]
    for ds in range(1, sections):
        same = same + R[2 * ds]
        other = other + R[2 * ds + 1]
    scale_same = 1.0 / jnp.sqrt(same / width_all + 1e-5)
    scale_other = 1.0 / jnp.sqrt(other / width_all + 1e-5)
    SC[core] = as_columns(scale_same)
    SC[1 - core] = as_columns(scale_other)
    copy_to(SB, XB.at[1 - core], one_s.at[0], one_r.at[0], sec, partner).wait_recv()

    for b in range(2):
        NP[8 + D * b : 8 + D * (b + 1), :] = XB[b, 0] * SC[b]
    rim = copy_to(NP.at[pl.ds(2 * D, 8)], RIM, one_s.at[1], one_r.at[1], sec, after)
    rim.start()

    r, c = iota2((D, D), 0), iota2((D, D), 1)
    incl = r >= c
    strict = r > c
    lower = jnp.where(incl, 1.0, 0.0).astype(BF16)
    fins = []
    for b in range(2):
        g = XB[b, 2]
        gh = g.astype(BF16)
        rest = g - gh.astype(F32)
        gm = rest.astype(BF16)
        gl = (rest - gm.astype(F32)).astype(BF16)
        cum = raw_dot(lower, gh, 1, 0) + (raw_dot(lower, gm, 1, 0) + raw_dot(lower, gl, 1, 0))
        mid = cum[D // 2 : D // 2 + 1]
        fin = cum[D - 1 : D]
        EX[b, 0] = jnp.exp(cum - mid)
        EX[b, 1] = jnp.exp(mid - cum)
        EX[b, 2] = jnp.exp(cum)
        EX[b, 3] = jnp.exp(fin - cum)
        fins.append(fin)

    copy_to(NP.at[pl.ds(2 * D, 8)], RIM, one_s.at[1], one_r.at[1], sec, before).wait_recv()
    NP[0:8, :] = jnp.where(chip == 0, 0.0, RIM[...])

    def tap(j, i):
        both = w_ref[j, i : i + 1, :]
        return jnp.where(first, both[:, :D], both[:, D:])

    taps = [[tap(j, i) for i in range(4)] for j in range(3)]
    shifted = [NP[5 + i : 5 + i + 2 * D, :] for i in range(4)]
    for j in range(3):
        mix = taps[j][0] * shifted[0]
        for i in range(1, 4):
            mix = mix + taps[j][i] * shifted[i]
        gate = 1.0 / (1.0 + jnp.exp(-mix))
        act = mix * gate
        slope = gate * (1.0 + mix * (1.0 - gate))
        if j < 2:
            norm = 1.0 / jnp.sqrt(jnp.sum(act * act, axis=1, keepdims=True) + 1e-6)
            QK[j] = act * norm
            DS[j] = slope * norm
        else:
            QK[j] = act
            DS[j] = slope

    blk = [slice(D * b, D * (b + 1)) for b in range(2)]
    systems, scores = [], []
    for b in range(2):
        q, k = QK[0, blk[b], :], QK[1, blk[b], :]
        kf, kb, qf = k * EX[b, 0], k * EX[b, 1], q * EX[b, 0]
        FB[b, 0:D, :] = kf
        FB[b, D : 2 * D, :] = qf
        FB[b, 2 * D : 3 * D, :] = kb
        both = mm_nt(jnp.concatenate([kf, qf], axis=0), kb)
        systems.append(jnp.where(strict, XB[b, 3] * both[:D], 0.0))
        scores.append(jnp.where(incl, both[D:], 0.0))
    inverses = unit_lower_inverse(systems)
    for b in range(2):
        q, k, v = QK[0, blk[b], :], QK[1, blk[b], :], QK[2, blk[b], :]
        beta, d_out, inv, sc = XB[b, 3], XB[b, 1], inverses[b], scores[b]
        ke, qc = k * EX[b, 3], q * EX[b, 2]
        wu = mm(inv, jnp.concatenate([beta * k * EX[b, 2], beta * v], axis=1))
        w, u = wu[:, :D], wu[:, D:]
        swu = mm(sc, wu)
        qeff = qc - swu[:, :D]
        WQ[b, 0:D, :] = w
        WQ[b, D : 2 * D, :] = qeff
        UO[b, 0] = u
        UO[b, 1] = swu[:, D:]
        MAPS[b, 0] = jnp.where(r == c, jnp.exp(fins[b]), 0.0) - mm_tn(ke, w)
        MAPS[b, 1] = mm_tn(u, ke)
        MAPS[b, 2] = mm_tn(d_out, qeff)
        h = mm_tn(sc, d_out)
        zk = mm_tn(inv, jnp.concatenate([h, ke], axis=1))
        ZK[b, 0] = zk[:, :D]
        ZK[b, 1] = zk[:, D:]

    t0, t1 = MAPS[0, 0], MAPS[1, 0]
    t_pair = mm(t1, t0)
    i_pair = mm_nt(MAPS[0, 1], t1) + MAPS[1, 1]
    s_pair = MAPS[0, 2] + mm(MAPS[1, 2], t0)
    TS[z] = t_pair
    for zz in range(n_z):
        VS[zz, 0:cols, :] = i_pair[zz * cols : (zz + 1) * cols]
        VS[zz, cols : 2 * cols, :] = s_pair[zz * cols : (zz + 1) * cols]
    VR[z] = VS[z]

    up_hops, down_hops = n_z // 2, n_z - 1 - n_z // 2

    def ring_copy(direction, hop):
        source = lax.rem(z + n_z - (hop - 1) if direction == 0 else z + hop - 1, n_z)
        target = lax.rem(z + 1 if direction == 0 else z + n_z - 1, n_z)
        slot = direction * up_hops + hop - 1
        return copy_to(TS.at[source], TS.at[source], ring_s.at[slot], ring_r.at[slot], sec, at_z(target))

    def ring_recv(direction, hop):
        source = lax.rem(z + n_z - hop if direction == 0 else z + hop, n_z)
        slot = direction * up_hops + hop - 1
        copy_to(TS.at[source], TS.at[source], ring_s.at[slot], ring_r.at[slot], sec, ctx).wait_recv()

    sent = []

    def go(copy):
        copy.start()
        sent.append(copy)

    go(ring_copy(0, 1))
    if down_hops:
        go(ring_copy(1, 1))
    for dz in range(1, n_z):
        to = lax.rem(z + dz, n_z)
        go(copy_to(VS.at[to], VR.at[z], vec_s.at[dz], vec_r.at[n_z - dz], sec, at_z(to)))
    for hop in range(1, up_hops + 1):
        ring_recv(0, hop)
        if hop < up_hops:
            go(ring_copy(0, hop + 1))
        if hop <= down_hops:
            ring_recv(1, hop)
            if hop < down_hops:
                go(ring_copy(1, hop + 1))
    for dz in range(1, n_z):
        src = lax.rem(z + dz, n_z)
        copy_to(VS.at[src], VR.at[src], vec_s.at[dz], vec_r.at[dz], sec, ctx).wait_recv()

    stack = jnp.concatenate([VR[0, 0:cols, :], jnp.transpose(TS[0])], axis=0)
    down = VR[n_z - 1, cols : 2 * cols, :]
    zero_map = jnp.zeros((D, D), F32)
    for step in range(1, n_z):
        zu, zd = step, n_z - 1 - step
        stack = mm_nt(stack, TS[zu]) + jnp.concatenate([VR[zu, 0:cols, :], zero_map], axis=0)
        down = mm(down, TS[zd]) + VR[zd, cols : 2 * cols, :]
    up, total = stack[:cols], stack[cols:]

    YB[0] = jnp.zeros((cols, D), F32)
    YB[1] = jnp.zeros((cols, D), F32)
    YB[2] = up
    YB[3] = down
    YB[4:4 + n_z, :, :] = total.reshape(n_z, cols, D)
    up_y = lax.rem(y + 1, n_y)
    down_y = lax.rem(y + n_y - 1, n_y)
    chain_up = copy_to(YB.at[2], SO.at[0, 0], one_s.at[2], one_r.at[2], sec, at_y(up_y))
    chain_down = copy_to(YB.at[3], SO.at[0, 1], one_s.at[3], one_r.at[3], sec, at_y(down_y))

    @pl.when(y > 0)
    def _():
        chain_up.wait_recv()
        arrived = SO[0, 0]
        YB[0] = arrived
        YB[2] = YB[2] + mm(arrived, YB[4:4 + n_z, :, :].reshape(D, D))

    @pl.when(y < n_y - 1)
    def _():
        chain_up.start()

    @pl.when(y < n_y - 1)
    def _():
        chain_down.wait_recv()
        arrived = SO[0, 1]
        YB[1] = arrived
        YB[3] = YB[3] + mm_nt(arrived, YB[4:4 + n_z, :, :].reshape(D, D))

    @pl.when(y > 0)
    def _():
        chain_down.start()

    up, down = YB[0], YB[1]

    def back_copy(zz, kind, to):
        slot = zz * 2 + kind
        return copy_to(SO.at[1 + zz, kind], ST.at[kind, pl.ds(pl.multiple_of(z * cols, cols), cols)],
                       back_s.at[slot], back_r.at[z * 2 + kind], sec, at_z(to))

    for step in range(n_z):
        zu, zd = step, n_z - 1 - step
        SO[1 + zu, 0] = up
        SO[1 + zd, 1] = down
        for zz, kind in ((zu, 0), (zd, 1)):
            @pl.when(z != zz)
            def _():
                back_copy(zz, kind, zz).start()

            @pl.when(z == zz)
            def _():
                ST[kind, zz * cols : (zz + 1) * cols, :] = SO[1 + zz, kind]
        if step < n_z - 1:
            up = mm_nt(up, TS[zu]) + VR[zu, 0:cols, :]
            down = mm(down, TS[zd]) + VR[zd, cols : 2 * cols, :]
    for dz in range(1, n_z):
        src = lax.rem(z + dz, n_z)
        for kind in range(2):
            copy_to(SO.at[1, kind], ST.at[kind, pl.ds(pl.multiple_of(src * cols, cols), cols)],
                    back_s.at[0], back_r.at[src * 2 + kind], sec, ctx).wait_recv()

    starts = [ST[0], None]
    ends = [None, ST[1]]
    starts[1] = mm_nt(starts[0], t0) + MAPS[0, 1]
    ends[0] = mm(ends[1], t1) + MAPS[1, 2]
    DM[:, 0:8, :] = jnp.zeros((3, 8, D), F32)
    DM[:, 8 + 2 * D :, :] = jnp.zeros((3, 8, D), F32)
    for b in range(2):
        q, k = QK[0, blk[b], :], QK[1, blk[b], :]
        beta, d_out = XB[b, 3], XB[b, 1]
        wq = mm_nt(WQ[b], starts[b])
        fresh = UO[b, 0] - wq[:D]
        OB[b] = UO[b, 1] + wq[D:]
        zeta = ZK[b, 0] + mm_nt(ZK[b, 1], ends[b])
        pair = mm_nt(jnp.concatenate([d_out, zeta], axis=0), fresh)
        d_sc = jnp.where(incl, pair[:D], 0.0)
        d_p = beta * jnp.where(strict, -pair[D:], 0.0)
        dz_s = mm(jnp.concatenate([d_out, zeta], axis=0), starts[b])
        f_g = mm(fresh, ends[b])
        by_kb = mm(jnp.concatenate([d_sc, d_p], axis=0), FB[b, 2 * D : 3 * D, :])
        d_kb = mm_tn(jnp.concatenate([d_p, d_sc], axis=0), FB[b, 0 : 2 * D, :])
        dq = EX[b, 2] * dz_s[:D] + EX[b, 0] * by_kb[:D]
        dk = EX[b, 3] * f_g - beta * EX[b, 2] * dz_s[D:] + EX[b, 0] * by_kb[D:] + EX[b, 1] * d_kb
        for j, (unit, grad) in enumerate(((q, dq), (k, dk))):
            along = jnp.sum(unit * grad, axis=1, keepdims=True)
            DM[j, 8 + D * b : 8 + D * (b + 1), :] = (grad - unit * along) * DS[j, blk[b], :]
        DM[2, 8 + D * b : 8 + D * (b + 1), :] = beta * zeta * DS[2, blk[b], :]
    out_swap = copy_to(OB.at[1 - core], OR, one_s.at[4], one_r.at[4], sec, partner)
    out_swap.start()

    d_norm = jnp.zeros((2 * D + 8, D), F32)
    for j in range(3):
        for i in range(4):
            d_norm = d_norm + taps[j][i] * DM[j, 3 - i : 3 - i + 2 * D + 8, :]
    RIMB[0] = d_norm[:8]
    rim_back = copy_to(RIMB.at[0], RIMB.at[1], one_s.at[5], one_r.at[5], sec, before)
    rim_back.start()
    GB[0] = d_norm[8 : 8 + D]
    GB[1] = d_norm[8 + D :]
    copy_to(RIMB.at[0], RIMB.at[1], one_s.at[5], one_r.at[5], sec, after).wait_recv()
    GB[1, D - 8 : D, :] = GB[1, D - 8 : D, :] + jnp.where(chip == n_ctx // 2 - 1, 0.0, RIMB[1])
    for b in range(2):
        TB[b] = row_sums(GB[b] * XB[b, 0])
    for ds, dc in peers:
        back = ((sections - ds) % sections) * 2 + dc
        copy = copy_to(TB.at[1 - core if dc else core], R2.at[back], row2_s.at[ds * 2 + dc], row2_r.at[back],
                       lax.rem(sec + ds, sections), partner if dc else ctx)
        go(copy)
    grad_swap = copy_to(GB.at[1 - core], GR, one_s.at[6], one_r.at[6], sec, partner)
    grad_swap.start()
    rows_wait(R2, row2_s, row2_r)
    inner = TB[core]
    for slot in range(1, 2 * sections):
        inner = inner + R2[slot]
    scale = SC[core]
    coef = as_columns(scale_same * scale_same * scale_same * inner / width_all)
    out_swap.wait_recv()
    grad_swap.wait_recv()

    def joined(own, oth):
        return jnp.concatenate([jnp.where(first, own, oth), jnp.where(first, oth, own)], axis=1)

    out_ref[...] = (x_ref[...].astype(F32) + joined(OB[core], OR[...])).astype(BF16)
    wide_scale = jnp.concatenate([scale, scale], axis=1)
    wide_coef = jnp.concatenate([coef, coef], axis=1)
    dx_ref[...] = (
        do_ref[...].astype(F32) + joined(GB[core], GR[...]) * wide_scale - x_ref[...].astype(F32) * wide_coef
    ).astype(BF16)

    for copy in row_copies + sent + [swap, rim, out_swap, rim_back, grad_swap]:
        copy.wait_send()

    @pl.when(y < n_y - 1)
    def _():
        chain_up.wait_send()

    @pl.when(y > 0)
    def _():
        chain_down.wait_send()

    for zz in range(n_z):
        @pl.when(z != zz)
        def _():
            for kind in range(2):
                back_copy(zz, kind, zz).wait_send()


def solution(mesh):
    sections, n_ctx = mesh.shape["section"], mesh.shape["ctx"]
    n_y, n_z = (4, 8) if n_ctx == 64 else (2, n_ctx // 4)
    cols = D // n_z
    dma = pltpu.SemaphoreType.DMA

    def shards(inputs, out_grads, conv_weight, log_decay, beta):
        width_all = float(inputs.shape[1] * sections)
        v = lambda *s: pltpu.VMEM(s, F32)
        scratch = [
            v(4, D, D), v(2, 4, D, D), v(2 * sections, 8, D), v(2 * sections, 8, D), v(2, 8, D),
            v(2 * D + 8, D), v(8, D), v(2, 8, D), v(2, D, D),
            v(3, 2 * D, D), v(3, 2 * D, D), v(2, 4, D, D), v(2, 3 * D, D), v(2, 2 * D, D), v(2, 2, D, D),
            v(2, 2, D, D), v(2, 3, D, D), v(n_z, D, D), v(n_z, 2 * cols, D), v(n_z, 2 * cols, D),
            v(4 + n_z, cols, D), v(1 + n_z, 2, cols, D), v(2, D, D), v(3, 2 * D + 16, D),
            v(2, D, D), v(D, D), v(2, D, D), v(D, D),
            dma((2 * sections,)), dma((2 * sections,)), dma((2 * sections,)), dma((2 * sections,)),
            dma((8,)), dma((8,)), dma((n_z,)), dma((n_z,)), dma((n_z,)), dma((n_z,)),
            dma((2 * n_z,)), dma((2 * n_z,)),
        ]
        vm = pl.BlockSpec(memory_space=pltpu.VMEM)
        return pl.pallas_call(
            functools.partial(kernel, (sections, n_y, n_z, width_all)),
            out_shape=(jax.ShapeDtypeStruct(inputs.shape, BF16), jax.ShapeDtypeStruct(inputs.shape, BF16)),
            in_specs=[vm] * 5,
            out_specs=(vm, vm),
            scratch_shapes=scratch,
            compiler_params=pltpu.CompilerParams(
                collective_id=0, has_side_effects=True, vmem_limit_bytes=40 * 2**20
            ),
        )(inputs, out_grads, log_decay, beta, conv_weight)

    spec = P("ctx", "section")
    return jax.shard_map(
        shards, mesh=mesh, in_specs=(spec, spec, P(None, None, "section"), spec, spec),
        out_specs=(spec, spec), check_vma=False,
    )
```

time: 700 us -> 87.2 us (0.12)
  waiting for transfers between devices: 491 us -> 0 us
  matrix products: 90.6 us -> 0 us
  Pallas kernels: 0 us -> 81.8 us
  blocking collectives: 56.8 us -> 0 us
  other arithmetic: 24.2 us -> 0 us
  between operations: 14.3 us -> 0.65 us
  starting transfers between devices: 11.9 us -> 0 us
    all_gather x4 -> x0, waiting for transfers between devices: 489 us -> none  [entering(): gathered = jax.tree.map(lambda a: lax.all_gather(a, axis), part)]
    dot_general x86 -> x0, matrix products: 89.6 us -> none  [the longest x63 78.2 us: compose(): jnp.einsum('hab,hbc->hac', second_map, first_add, precision=highest)]
    pallas_call x0 -> x1, Pallas kernels: none -> 81.8 us  [shards(): pl.pallas_call(functools.partial(kernel, (sections, n_y, n_z, width_all))...]
    psum x2 -> x0, blocking collectives: 56.8 us -> none  [section_sum(): return lax.psum(values, 'section')]
    another operation x5 -> x0, other arithmetic: 19.9 us -> none  [the longest x4 19.8 us: solve_block(): lax.linalg.triangular_solve(system, jnp.concatenate([rhs_keys, rhs_values...]
    ppermute x2 -> x0, starting transfers between devices: 11.8 us -> none  [passed_along(): return lax.ppermute(block, axis, route)]
  transfers between devices with their start and end apart: 6 -> 0, of which waited for: 5 -> 0; matrix products, arithmetic and copies ran while one was open for 2% -> 0% of each run, Pallas kernels for 0% -> 0%
where the time goes in v1:
time: 87.2 us; the launch traced here: 87 us
  Pallas kernels  81.8 us (94%)
  local copies, waits for them, and re-layouts  4.54 us (5%)
    pallas_call x1, Pallas kernels, shards(): pl.pallas_call(functools.partial(kernel, (sections, n_y, n_z, width_all))...  81.8 us
    unnamed x11, local copies, waits for them, and re-layouts  4.54 us

profile of v1, /device:TPU:1, one launch (start us, length us, event | category | flops | bytes accessed | tf_op | source)
XLA Modules:
  0.0 87.0 jit_solution(13209711143310726655)
XLA Ops:
  0.6 0.0 copy-start.1
  0.6 0.8 copy.7.beta_ref
  1.5 0.0 copy-done.1
  1.5 0.0 copy-start
  1.5 0.9 %copy-done = f32[128,256]{1,0:T(8,128)S(1)} copy-done((f32[128,256]{1,0:T(8,128)S(1)}, f32[128,256]{1,0:T(8,128)}, u32[]{:S(2)}) %copy-start) | copy-done | bytes 131096
  2.4 0.0 copy-start.2
  2.4 0.8 copy-done.2
  3.2 0.0 copy-start.3
  3.2 0.7 copy-done.3
  3.9 81.8 %shard_map.68 = (bf16[128,256]{1,0:T(8,128)(2,1)S(1)}, bf16[128,256]{1,0:T(8,128)(2,1)S(1)}) custom-call(bf16[128,256]{1,0:T(8,128)(2,1)S(1)} %copy-done.1, bf16[128,256]{1,0:T(8,128)(2,1)S(1)} %copy-done.2, f32[128,256]{1,0:T(8,128)S(1)} %copy-done, f32[128,2]{1,0:T(8,128)S(1)} %copy.7.beta_ref, f32[3,4,256]{2,1,0:T(4,128)S(1)} %copy-done.3), custom_call_target="tpu_custom_call" | custom-call | tf_op jit(solution)/shard_map/pallas_call | solution.py:471
  85.7 0.6 copy.10
  86.3 0.6 copy.11
Async XLA Ops:
  0.6 0.8 copy-start.1
  1.5 0.9 %copy-start = (f32[128,256]{1,0:T(8,128)S(1)}, f32[128,256]{1,0:T(8,128)}, u32[]{:S(2)}) copy-start(f32[128,256]{1,0:T(8,128)} %g_ref.1) | copy-start | bytes 393220
  2.4 0.8 copy-start.2
  3.2 0.7 copy-start.3

commit v2 on v1

v2 whole, which is shorter than its diff:
```python
import functools

import jax
import jax.numpy as jnp
from jax import lax
from jax.experimental import pallas as pl
from jax.experimental.pallas import tpu as pltpu
from jax.sharding import PartitionSpec as P

MESH = pl.DeviceIdType.MESH
D = 128
F32 = jnp.float32
BF16 = jnp.bfloat16


def split2(a):
    high = a.astype(BF16)
    low = (a - high.astype(F32)).astype(BF16)
    return high, low


def raw_dot(a, b, ca, cb):
    return lax.dot_general(a, b, (((ca,), (cb,)), ((), ())), preferred_element_type=F32)


def mm(a, b, ca=1, cb=0):
    ah, al = split2(a)
    bh, bl = split2(b)
    return raw_dot(ah, bh, ca, cb) + (raw_dot(ah, bl, ca, cb) + raw_dot(al, bh, ca, cb))


def mm_nt(a, b):
    return mm(a, b, 1, 1)


def mm_tn(a, b):
    return mm(a, b, 0, 0)


def iota2(shape, axis):
    return lax.broadcasted_iota(jnp.int32, shape, axis)


def row_sums(values):
    high, low = split2(values)
    ones = jnp.ones((8, values.shape[1]), BF16)
    return raw_dot(ones, high, 1, 1) + raw_dot(ones, low, 1, 1)


def as_columns(tile):
    return jnp.transpose(jnp.broadcast_to(tile[0:1], (D, D)))


def unit_lower_inverse(strict_parts):
    r, c = iota2((D, D), 0), iota2((D, D), 1)
    eye = jnp.where(r == c, 1.0, 0.0).astype(F32)
    inverse = None
    for k in range(7):
        mask = ((r >> (k + 1)) == (c >> (k + 1))) & (((r >> k) & 1) == 1) & (((c >> k) & 1) == 0)
        off = [jnp.where(mask, a, 0.0) for a in strict_parts]
        if k == 0:
            inverse = [eye - o for o in off]
        else:
            half = [mm(m, o) for m, o in zip(inverse, off)]
            inverse = [m - mm(h, m) for h, m in zip(half, inverse)]
    return inverse


def kernel(geom, x_hbm, do_hbm, g_hbm, beta_hbm, w_hbm, out_ref, dx_ref, *scratch):
    sections, n_y, n_z, width_all = geom
    (
        x_ref, do_ref, g_ref, beta_ref, w_ref,
        SB, XB, R, R2, TB, NP, RIM, RIMR, SC, GRIM, RIM2, RT,
        QK, DS, EX, FB, WQ, UO, ZK, MAPS, TS, VS, VR, UP, DN, XS, XF, XY, PY, SG, SGF, DM, OB, OR, GB, GR,
        in_s, row_s, row_r, rim_s, rim_r, row2_s, row2_r, rim2_s, rim2_r, one_s, one_r,
        ring_s, ring_r, vec_s, vec_r, xf_s, xf_r, sg_s, sg_r, ya_s, ya_r, yb_s, yb_r,
    ) = scratch
    n_ctx = n_y * n_z * 2
    n_chip = n_y * n_z
    cols = D // n_z
    half = n_z // 2
    sec = lax.axis_index("section")
    ctx = lax.axis_index("ctx")
    core = lax.rem(ctx, 2)
    chip = ctx // 2
    y = chip // n_z
    z = lax.rem(chip, n_z)
    partner = ctx + 1 - 2 * core
    first = core == 0
    has_before = chip > 0
    has_after = chip < n_chip - 1
    feeds = jnp.logical_and(core == 1, has_after)
    after_chip = 2 * lax.rem(chip + 1, n_chip)
    before_tail = 2 * lax.rem(chip + n_chip - 1, n_chip) + 1

    def at_z(zz):
        return y * (2 * n_z) + zz * 2 + core

    def at_y(yy):
        return yy * (2 * n_z) + z * 2 + core

    def side(ds):
        return lax.rem(sec + ds, sections)

    def copy_to(src, dst, ss, rs, to_sec, to_ctx):
        return pltpu.make_async_remote_copy(
            src_ref=src, dst_ref=dst, send_sem=ss, recv_sem=rs,
            device_id=(to_sec, to_ctx), device_id_type=MESH,
        )

    def arrives(dst, rs):
        copy_to(dst, dst, one_s.at[0], rs, sec, partner).wait_recv()

    sent = []

    def go(*args):
        copy = copy_to(*args)
        copy.start()
        sent.append(copy)

    peers = [(ds, dc) for ds in range(sections) for dc in range(2) if ds or dc]

    loads = [
        pltpu.make_async_copy(src, dst, in_s.at[n])
        for n, (src, dst) in enumerate(
            ((x_hbm, x_ref), (do_hbm, do_ref), (g_hbm, g_ref), (beta_hbm, beta_ref), (w_hbm, w_ref))
        )
    ]
    for load in loads:
        load.start()

    barrier = pltpu.get_barrier_semaphore()

    def greet(to_sec, to_ctx):
        pl.semaphore_signal(barrier, inc=1, device_id=(to_sec, to_ctx), device_id_type=MESH)

    for ds, dc in peers:
        greet(side(ds), partner if dc else ctx)
    for dz in range(1, n_z):
        greet(sec, at_z(lax.rem(z + dz, n_z)))
    for dy in range(1, n_y):
        greet(sec, at_y(lax.rem(y + dy, n_y)))

    @pl.when(has_before)
    def _():
        for ds in range(sections):
            greet(side(ds), before_tail)

    @pl.when(feeds)
    def _():
        for ds in range(sections):
            for dc in range(2):
                greet(side(ds), after_chip + dc)

    greeted = (
        len(peers) + n_z - 1 + n_y - 1
        + sections * has_before.astype(jnp.int32) + 2 * sections * feeds.astype(jnp.int32)
    )

    for load in loads:
        load.wait()

    def halves(ref):
        whole = ref[...].astype(F32)
        low, high = whole[:, :D], whole[:, D:]
        return jnp.where(first, low, high), jnp.where(first, high, low), whole

    x_own, x_oth, x_all = halves(x_ref)
    R[0] = row_sums(x_all * x_all)
    d_own, d_oth, _ = halves(do_ref)
    g_own, g_oth, _ = halves(g_ref)
    b0, b1 = as_columns(beta_ref[0:1, :]), as_columns(beta_ref[1:2, :])
    SB[0] = x_oth
    SB[1] = d_oth
    SB[2] = g_oth
    SB[3] = jnp.where(first, b1, b0)
    XB[core, 0] = x_own
    XB[core, 1] = d_own
    XB[core, 2] = g_own
    XB[core, 3] = jnp.where(first, b0, b1)
    RT[0] = x_all[D - 8 :, :D]
    RT[1] = x_all[D - 8 :, D:]
    pl.semaphore_wait(barrier, greeted)

    for ds, dc in reversed(peers):
        back = ((sections - ds) % sections) * 2 + dc
        go(R.at[0], R.at[back], row_s.at[ds * 2 + dc], row_r.at[back], side(ds), partner if dc else ctx)
    go(SB, XB.at[core], one_s.at[0], one_r.at[0], sec, partner)

    def rim_copies():
        made = []
        for dc in range(2):
            made.append(copy_to(RT.at[dc], RIMR, rim_s.at[2 * sections + dc], rim_r.at[sections], sec, after_chip + dc))
            for ds in range(sections):
                made.append(copy_to(R.at[0], RIM.at[(sections - ds) % sections], rim_s.at[2 * ds + dc],
                                    rim_r.at[(sections - ds) % sections], side(ds), after_chip + dc))
        return made

    @pl.when(feeds)
    def _():
        for copy in rim_copies():
            copy.start()

    arrives(XB.at[1 - core], one_r.at[0])
    r, c = iota2((D, D), 0), iota2((D, D), 1)
    incl = r >= c
    strict = r > c
    lower = jnp.where(incl, 1.0, 0.0).astype(BF16)
    fins = []
    for b in range(2):
        g = XB[b, 2]
        gh = g.astype(BF16)
        rest = g - gh.astype(F32)
        gm = rest.astype(BF16)
        gl = (rest - gm.astype(F32)).astype(BF16)
        cum = raw_dot(lower, gh, 1, 0) + (raw_dot(lower, gm, 1, 0) + raw_dot(lower, gl, 1, 0))
        mid = cum[D // 2 : D // 2 + 1]
        fin = cum[D - 1 : D]
        EX[b, 0] = jnp.exp(cum - mid)
        EX[b, 1] = jnp.exp(mid - cum)
        EX[b, 2] = jnp.exp(cum)
        EX[b, 3] = jnp.exp(fin - cum)
        fins.append(fin)

    for ds, dc in peers:
        slot = ds * 2 + dc
        arrives(R.at[slot], row_r.at[slot])
    same = R[0]
    other = R[1]
    for ds in range(1, sections):
        same = same + R[2 * ds]
        other = other + R[2 * ds + 1]

    def scale_of(total):
        return 1.0 / jnp.sqrt(total / width_all + 1e-5)

    scale_same = scale_of(same)
    SC[core] = as_columns(scale_same)
    SC[1 - core] = as_columns(scale_of(other))
    for b in range(2):
        NP[8 + D * b : 8 + D * (b + 1), :] = XB[b, 0] * SC[b]

    @pl.when(has_before)
    def _():
        for ds in range(sections):
            arrives(RIM.at[ds], rim_r.at[ds])
        arrives(RIMR, rim_r.at[sections])
        rim_total = RIM[0]
        for ds in range(1, sections):
            rim_total = rim_total + RIM[ds]
        NP[0:8, :] = RIMR[...] * as_columns(scale_of(rim_total))[D - 8 :]

    @pl.when(jnp.logical_not(has_before))
    def _():
        NP[0:8, :] = jnp.zeros((8, D), F32)
        RIMR[...] = jnp.zeros((8, D), F32)

    def tap(j, i):
        both = w_ref[j, i : i + 1, :]
        return jnp.where(first, both[:, :D], both[:, D:])

    taps = [[tap(j, i) for i in range(4)] for j in range(3)]
    shifted = [NP[5 + i : 5 + i + 2 * D, :] for i in range(4)]
    for j in range(3):
        mix = taps[j][0] * shifted[0]
        for i in range(1, 4):
            mix = mix + taps[j][i] * shifted[i]
        gate = 1.0 / (1.0 + jnp.exp(-mix))
        act = mix * gate
        slope = gate * (1.0 + mix * (1.0 - gate))
        if j < 2:
            norm = 1.0 / jnp.sqrt(jnp.sum(act * act, axis=1, keepdims=True) + 1e-6)
            QK[j] = act * norm
            DS[j] = slope * norm
        else:
            QK[j] = act
            DS[j] = slope

    blk = [slice(D * b, D * (b + 1)) for b in range(2)]
    systems, scores = [], []
    for b in range(2):
        q, k = QK[0, blk[b], :], QK[1, blk[b], :]
        kf, kb, qf = k * EX[b, 0], k * EX[b, 1], q * EX[b, 0]
        FB[b, 0:D, :] = kf
        FB[b, D : 2 * D, :] = qf
        FB[b, 2 * D : 3 * D, :] = kb
        both = mm_nt(jnp.concatenate([kf, qf], axis=0), kb)
        systems.append(jnp.where(strict, XB[b, 3] * both[:D], 0.0))
        scores.append(jnp.where(incl, both[D:], 0.0))
    inverses = unit_lower_inverse(systems)
    wus, kes = [], []
    for b in range(2):
        k, v, beta = QK[1, blk[b], :], QK[2, blk[b], :], XB[b, 3]
        ke = k * EX[b, 3]
        wu = mm(inverses[b], jnp.concatenate([beta * k * EX[b, 2], beta * v], axis=1))
        MAPS[b, 0] = jnp.where(r == c, jnp.exp(fins[b]), 0.0) - mm_tn(ke, wu[:, :D])
        wus.append(wu)
        kes.append(ke)
    t0, t1 = MAPS[0, 0], MAPS[1, 0]
    TS[z] = mm(t1, t0)

    direct = [dz for dz in range(1, n_z) if dz != half or n_z == 2]
    for dz in sorted(direct, key=lambda dz: (min(dz, n_z - dz) > 1, -min(dz, n_z - dz))):
        go(TS.at[z], TS.at[z], ring_s.at[dz], ring_r.at[n_z - dz], sec, at_z(lax.rem(z + dz, n_z)))

    for b in range(2):
        q, d_out, sc = QK[0, blk[b], :], XB[b, 1], scores[b]
        w, u = wus[b][:, :D], wus[b][:, D:]
        swu = mm(sc, wus[b])
        qeff = q * EX[b, 2] - swu[:, :D]
        WQ[b, 0:D, :] = w
        WQ[b, D : 2 * D, :] = qeff
        UO[b, 0] = u
        UO[b, 1] = swu[:, D:]
        MAPS[b, 1] = mm_tn(u, kes[b])
        MAPS[b, 2] = mm_tn(d_out, qeff)
    i_pair = mm_nt(MAPS[0, 1], t1) + MAPS[1, 1]
    s_pair = MAPS[0, 2] + mm(MAPS[1, 2], t0)
    for zz in range(n_z):
        VS[zz, 0:cols, :] = i_pair[zz * cols : (zz + 1) * cols]
        VS[zz, cols : 2 * cols, :] = s_pair[zz * cols : (zz + 1) * cols]
    VR[z] = VS[z]
    for dz in range(1, n_z):
        to = lax.rem(z + dz, n_z)
        go(VS.at[to], VR.at[z], vec_s.at[dz], vec_r.at[n_z - dz], sec, at_z(to))
    if n_z > 2:
        low, high = pl.ds(0, D // 2), pl.ds(D // 2, D // 2)
        left, right = lax.rem(z + n_z - 1, n_z), lax.rem(z + 1, n_z)
        arrives(TS.at[left], ring_r.at[n_z - 1])
        go(TS.at[left, low], TS.at[left, low], ring_s.at[0], ring_r.at[0], sec, at_z(lax.rem(z + half - 1, n_z)))
        arrives(TS.at[right], ring_r.at[1])
        go(TS.at[right, high], TS.at[right, high], ring_s.at[half], ring_r.at[half], sec,
           at_z(lax.rem(z + n_z - half + 1, n_z)))

    for b in range(2):
        h = mm_tn(scores[b], XB[b, 1])
        zk = mm_tn(inverses[b], jnp.concatenate([h, kes[b]], axis=1))
        ZK[b, 0] = zk[:, :D]
        ZK[b, 1] = zk[:, D:]
    for dz in direct:
        if n_z == 2 or dz not in (1, n_z - 1):
            arrives(TS.at[lax.rem(z + dz, n_z)], ring_r.at[dz])
    for dz in range(1, n_z):
        arrives(VR.at[lax.rem(z + dz, n_z)], vec_r.at[dz])
    if n_z > 2:
        far = lax.rem(z + half, n_z)
        arrives(TS.at[far, low], ring_r.at[0])
        arrives(TS.at[far, high], ring_r.at[half])

    eye = jnp.where(r == c, 1.0, 0.0).astype(F32)
    zero_map = jnp.zeros((D, D), F32)
    UP[0] = jnp.concatenate([jnp.zeros((cols, D), F32), eye], axis=0)
    DN[n_z - 1] = jnp.concatenate([jnp.zeros((cols, D), F32), eye], axis=0)
    up = jnp.concatenate([VR[0, 0:cols, :], jnp.transpose(TS[0])], axis=0)
    down = jnp.concatenate([VR[n_z - 1, cols : 2 * cols, :], TS[n_z - 1]], axis=0)
    for step in range(1, n_z):
        zu, zd = step, n_z - 1 - step
        UP[zu] = up
        DN[zd] = down
        up = mm_nt(up, TS[zu]) + jnp.concatenate([VR[zu, 0:cols, :], zero_map], axis=0)
        down = mm(down, TS[zd]) + jnp.concatenate([VR[zd, cols : 2 * cols, :], zero_map], axis=0)
    XY[y, 0] = up[:cols]
    XY[y, 1] = down[:cols]
    for dy in range(1, n_y):
        go(XY.at[y], XY.at[y], ya_s.at[dy], ya_r.at[n_y - dy], sec, at_y(lax.rem(y + dy, n_y)))

    def map_copy(yy, dy):
        slot = PY.at[yy - 1]
        return copy_to(slot, slot, yb_s.at[dy], yb_r.at[yy], sec, at_y(lax.rem(y + dy, n_y)))

    for yy in range(1, n_y - 1):
        @pl.when(y == yy)
        def _():
            PY[yy - 1] = up[cols:]
            for dy in range(1, n_y):
                map_copy(yy, dy).start()

    for zz in range(n_z):
        XS[zz, 0] = UP[zz, 0:cols, :]
        XS[zz, 1] = DN[zz, 0:cols, :]
    mine = pl.ds(pl.multiple_of(z * cols, cols), cols)
    XF[:, mine, :] = XS[z]
    for dz in range(1, n_z):
        to = lax.rem(z + dz, n_z)
        go(XS.at[to], XF.at[:, mine], xf_s.at[dz], xf_r.at[n_z - dz], sec, at_z(to))

    for dy in range(1, n_y):
        arrives(XY.at[lax.rem(y + dy, n_y)], ya_r.at[dy])
    for yy in range(1, n_y - 1):
        @pl.when(y != yy)
        def _():
            arrives(PY.at[yy - 1], yb_r.at[yy])
    enter = jnp.where(y > 0, XY[0, 0], 0.0)
    leave = jnp.where(y < n_y - 1, XY[n_y - 1, 1], 0.0)
    for step in range(1, n_y - 1):
        yu, yd = step, n_y - 1 - step
        enter = jnp.where(y > yu, mm(enter, PY[yu - 1]) + XY[yu, 0], enter)
        leave = jnp.where(y < yd, mm_nt(leave, PY[yd - 1]) + XY[yd, 1], leave)
    SG[0] = enter
    SG[1] = leave
    SGF[:, mine, :] = SG[...]
    for dz in range(1, n_z):
        go(SG, SGF.at[:, mine], sg_s.at[dz], sg_r.at[n_z - dz], sec, at_z(lax.rem(z + dz, n_z)))
    for dz in range(1, n_z):
        theirs = pl.ds(pl.multiple_of(lax.rem(z + dz, n_z) * cols, cols), cols)
        arrives(XF.at[:, theirs], xf_r.at[dz])
        arrives(SGF.at[:, theirs], sg_r.at[dz])

    starts = [XF[0] + mm(SGF[0], UP[z, cols:, :]), None]
    ends = [None, XF[1] + mm(SGF[1], DN[z, cols:, :])]
    starts[1] = mm_nt(starts[0], t0) + MAPS[0, 1]
    ends[0] = mm(ends[1], t1) + MAPS[1, 2]
    DM[:, 0:8, :] = jnp.zeros((3, 8, D), F32)
    DM[:, 8 + 2 * D :, :] = jnp.zeros((3, 8, D), F32)
    for b in range(2):
        q, k = QK[0, blk[b], :], QK[1, blk[b], :]
        beta, d_out = XB[b, 3], XB[b, 1]
        wq = mm_nt(WQ[b], starts[b])
        fresh = UO[b, 0] - wq[:D]
        OB[b] = UO[b, 1] + wq[D:]
        zeta = ZK[b, 0] + mm_nt(ZK[b, 1], ends[b])
        pair = mm_nt(jnp.concatenate([d_out, zeta], axis=0), fresh)
        d_sc = jnp.where(incl, pair[:D], 0.0)
        d_p = beta * jnp.where(strict, -pair[D:], 0.0)
        dz_s = mm(jnp.concatenate([d_out, zeta], axis=0), starts[b])
        f_g = mm(fresh, ends[b])
        by_kb = mm(jnp.concatenate([d_sc, d_p], axis=0), FB[b, 2 * D : 3 * D, :])
        d_kb = mm_tn(jnp.concatenate([d_p, d_sc], axis=0), FB[b, 0 : 2 * D, :])
        dq = EX[b, 2] * dz_s[:D] + EX[b, 0] * by_kb[:D]
        dk = EX[b, 3] * f_g - beta * EX[b, 2] * dz_s[D:] + EX[b, 0] * by_kb[D:] + EX[b, 1] * d_kb
        for j, (unit, grad) in enumerate(((q, dq), (k, dk))):
            along = jnp.sum(unit * grad, axis=1, keepdims=True)
            DM[j, 8 + D * b : 8 + D * (b + 1), :] = (grad - unit * along) * DS[j, blk[b], :]
        DM[2, 8 + D * b : 8 + D * (b + 1), :] = beta * zeta * DS[2, blk[b], :]
    go(OB.at[1 - core], OR, one_s.at[1], one_r.at[1], sec, partner)

    d_norm = jnp.zeros((2 * D + 8, D), F32)
    for j in range(3):
        for i in range(4):
            d_norm = d_norm + taps[j][i] * DM[j, 3 - i : 3 - i + 2 * D + 8, :]
    GB[0] = d_norm[8 : 8 + D]
    GB[1] = d_norm[8 + D :]
    GRIM[2] = d_norm[:8]
    TB[2] = row_sums(jnp.concatenate([jnp.zeros((D - 8, D), F32), d_norm[:8] * RIMR[...]], axis=0))
    TB[0] = row_sums(d_norm[8 : 8 + D] * XB[0, 0])
    TB[1] = row_sums(d_norm[8 + D :] * XB[1, 0])

    for ds, dc in reversed(peers):
        back = ((sections - ds) % sections) * 2 + dc
        go(TB.at[1 - core if dc else core], R2.at[back], row2_s.at[ds * 2 + dc], row2_r.at[back],
           side(ds), partner if dc else ctx)

    def rim_back_copies():
        made = [copy_to(GRIM.at[2], GRIM.at[core], rim2_s.at[sections], rim2_r.at[2 * sections + core], sec, before_tail)]
        for ds in range(sections):
            slot = 2 * ((sections - ds) % sections) + core
            made.append(copy_to(TB.at[2], RIM2.at[slot], rim2_s.at[ds], rim2_r.at[slot], side(ds), before_tail))
        return made

    @pl.when(has_before)
    def _():
        for copy in rim_back_copies():
            copy.start()

    go(GB.at[1 - core], GR, one_s.at[2], one_r.at[2], sec, partner)

    @pl.when(feeds)
    def _():
        for slot in range(2 * sections):
            arrives(RIM2.at[slot], rim2_r.at[slot])
        for n in range(2):
            arrives(GRIM.at[n], rim2_r.at[2 * sections + n])

    @pl.when(jnp.logical_not(feeds))
    def _():
        RIM2[...] = jnp.zeros((2 * sections, 8, D), F32)
        GRIM[0] = jnp.zeros((8, D), F32)
        GRIM[1] = jnp.zeros((8, D), F32)

    for ds, dc in peers:
        slot = ds * 2 + dc
        arrives(R2.at[slot], row2_r.at[slot])
    inner = TB[core] + RIM2[0]
    for slot in range(1, 2 * sections):
        inner = inner + R2[slot] + RIM2[slot]
    scale = SC[core]
    coef = as_columns(scale_same * scale_same * scale_same * inner / width_all)
    arrives(OR, one_r.at[1])
    arrives(GR, one_r.at[2])

    def joined(own, oth):
        return jnp.concatenate([jnp.where(first, own, oth), jnp.where(first, oth, own)], axis=1)

    out_ref[...] = (x_ref[...].astype(F32) + joined(OB[core], OR[...])).astype(BF16)
    late = jnp.concatenate([GRIM[0], GRIM[1]], axis=1)
    grads = joined(GB[core], GR[...])
    grads = jnp.concatenate([grads[: D - 8], grads[D - 8 :] + late], axis=0)
    wide_scale = jnp.concatenate([scale, scale], axis=1)
    wide_coef = jnp.concatenate([coef, coef], axis=1)
    dx_ref[...] = (
        do_ref[...].astype(F32) + grads * wide_scale - x_ref[...].astype(F32) * wide_coef
    ).astype(BF16)

    for copy in sent:
        copy.wait_send()

    @pl.when(feeds)
    def _():
        for copy in rim_copies():
            copy.wait_send()

    @pl.when(has_before)
    def _():
        for copy in rim_back_copies():
            copy.wait_send()

    for yy in range(1, n_y - 1):
        @pl.when(y == yy)
        def _():
            for dy in range(1, n_y):
                map_copy(yy, dy).wait_send()


def solution(mesh):
    sections, n_ctx = mesh.shape["section"], mesh.shape["ctx"]
    n_y, n_z = (4, 8) if n_ctx == 64 else (2, n_ctx // 4)
    cols = D // n_z
    dma = lambda n: pltpu.SemaphoreType.DMA((n,))

    def shards(inputs, out_grads, conv_weight, log_decay, beta):
        width_all = float(inputs.shape[1] * sections)
        v = lambda *s: pltpu.VMEM(s, F32)
        scratch = [
            pltpu.VMEM((D, 2 * D), BF16), pltpu.VMEM((D, 2 * D), BF16), v(D, 2 * D), v(2, D), v(3, 4, 2 * D),
            v(4, D, D), v(2, 4, D, D), v(2 * sections, 8, D), v(2 * sections, 8, D), v(3, 8, D),
            v(2 * D + 8, D), v(sections, 8, D), v(8, D), v(2, D, D), v(3, 8, D), v(2 * sections, 8, D), v(2, 8, D),
            v(3, 2 * D, D), v(3, 2 * D, D), v(2, 4, D, D), v(2, 3 * D, D), v(2, 2 * D, D), v(2, 2, D, D),
            v(2, 2, D, D), v(2, 3, D, D), v(n_z, D, D), v(n_z, 2 * cols, D), v(n_z, 2 * cols, D),
            v(n_z, cols + D, D), v(n_z, cols + D, D), v(n_z, 2, cols, D), v(2, D, D), v(n_y, 2, cols, D),
            v(max(n_y - 2, 1), D, D), v(2, cols, D), v(2, D, D), v(3, 2 * D + 16, D),
            v(2, D, D), v(D, D), v(2, D, D), v(D, D),
            dma(5), dma(2 * sections), dma(2 * sections), dma(2 * sections + 2), dma(sections + 1),
            dma(2 * sections), dma(2 * sections), dma(sections + 1), dma(2 * sections + 2), dma(3), dma(3),
            dma(n_z), dma(n_z), dma(n_z), dma(n_z), dma(n_z), dma(n_z), dma(n_z), dma(n_z),
            dma(n_y), dma(n_y), dma(n_y), dma(n_y),
        ]
        vm = pl.BlockSpec(memory_space=pltpu.VMEM)
        hbm = pl.BlockSpec(memory_space=pltpu.MemorySpace.HBM)
        return pl.pallas_call(
            functools.partial(kernel, (sections, n_y, n_z, width_all)),
            out_shape=(jax.ShapeDtypeStruct(inputs.shape, BF16), jax.ShapeDtypeStruct(inputs.shape, BF16)),
            in_specs=[hbm] * 5,
            out_specs=(vm, vm),
            scratch_shapes=scratch,
            compiler_params=pltpu.CompilerParams(
                collective_id=0, has_side_effects=True, vmem_limit_bytes=64 * 2**20 - 2**18
            ),
        )(inputs, out_grads, log_decay, beta.T, conv_weight)

    spec = P("ctx", "section")
    return jax.shard_map(
        shards, mesh=mesh, in_specs=(spec, spec, P(None, None, "section"), spec, spec),
        out_specs=(spec, spec), check_vma=False,
    )
```

time: 87.2 us -> 71.1 us (0.82)
  Pallas kernels: 81.8 us -> 68.1 us
  local copies, waits for them, and re-layouts: 4.54 us -> 2.14 us
    pallas_call x1, Pallas kernels: 81.8 us -> 68.1 us  [shards(): pl.pallas_call(functools.partial(kernel, (sections, n_y, n_z, width_all))...]
    unnamed x11 -> x4, local copies, waits for them, and re-layouts: 4.54 us -> 2.14 us
where the time goes in v2:
time: 71.1 us; the launch traced here: 70.9 us
  Pallas kernels  68.1 us (96%)
  local copies, waits for them, and re-layouts  2.14 us (3%)
    pallas_call x1, Pallas kernels, shards(): pl.pallas_call(functools.partial(kernel, (sections, n_y, n_z, width_all))...  68.1 us
    unnamed x4, local copies, waits for them, and re-layouts  2.14 us

profile of v2, /device:TPU:1, one launch (start us, length us, event | category | flops | bytes accessed | tf_op | source)
XLA Modules:
  0.0 70.9 jit_solution(8516160316523107327)
XLA Ops:
  0.6 68.1 %shard_map.68 = (bf16[128,256]{1,0:T(8,128)(2,1)}, bf16[128,256]{1,0:T(8,128)(2,1)}) custom-call(bf16[128,256]{1,0:T(8,128)(2,1)} %x_hbm.1, bf16[128,256]{1,0:T(8,128)(2,1)} %do_hbm.1, f32[128,256]{1,0:T(8,128)} %g_hbm.1, f32[2,128]{1,0:T(2,128)} %bitcast.1, f32[3,4,256]{2,1,0:T(4,128)} %w_hbm.1), custom_call_target="tpu_custom_call" | custom-call | tf_op jit(solution)/shard_map/pallas_call | solution.py:549
  68.8 0.0 copy-start
  68.8 1.5 %copy.9 = bf16[128,256]{1,0:T(8,128)(2,1)} copy(bf16[128,256]{1,0:T(8,128)(2,1)} %get-tuple-element.4) | data formatting | bytes 131072
  70.3 0.0 copy-done
  70.3 0.6 copy.10
Async XLA Ops:
  68.8 1.5 %copy-start = (bf16[128,256]{1,0:T(8,128)(2,1)S(1)}, bf16[128,256]{1,0:T(8,128)(2,1)}, u32[]{:S(2)}) copy-start(bf16[128,256]{1,0:T(8,128)(2,1)} %get-tuple-element.5) | copy-start | bytes 196612

commit v3 on v2

--- a/solution.py
+++ b/solution.py
@@ -26,7 +26,11 @@
 def mm(a, b, ca=1, cb=0):
     ah, al = split2(a)
     bh, bl = split2(b)
-    return raw_dot(ah, bh, ca, cb) + (raw_dot(ah, bl, ca, cb) + raw_dot(al, bh, ca, cb))
+    aa = jnp.concatenate([ah, al], axis=ca)
+    bb = jnp.concatenate([jnp.concatenate([bh, bh], axis=cb), jnp.concatenate([bl, bl], axis=cb)], axis=1 - cb)
+    wide = raw_dot(aa, bb, ca, cb)
+    n = b.shape[1 - cb]
+    return wide[:, :n] + wide[:, n:]
 
 
 def mm_nt(a, b):
@@ -71,14 +75,14 @@
     (
         x_ref, do_ref, g_ref, beta_ref, w_ref,
         SB, XB, R, R2, TB, NP, RIM, RIMR, SC, GRIM, RIM2, RT,
-        QK, DS, EX, FB, WQ, UO, ZK, MAPS, TS, VS, VR, UP, DN, XS, XF, XY, PY, SG, SGF, DM, OB, OR, GB, GR,
+        QK, DS, EX, FB, WQ, UO, ZK, MAPS, TS, VS, VR, UP, DN, XY, PY, SS, ST, DM, OB, OR, GB, GR,
         in_s, row_s, row_r, rim_s, rim_r, row2_s, row2_r, rim2_s, rim2_r, one_s, one_r,
-        ring_s, ring_r, vec_s, vec_r, xf_s, xf_r, sg_s, sg_r, ya_s, ya_r, yb_s, yb_r,
+        ring_s, ring_r, vec_s, vec_r, sg_s, sg_r, ya_s, ya_r, yb_s, yb_r,
     ) = scratch
     n_ctx = n_y * n_z * 2
     n_chip = n_y * n_z
-    cols = D // n_z
-    half = n_z // 2
+    roots = n_z // 2
+    cols = D // roots
     sec = lax.axis_index("section")
     ctx = lax.axis_index("ctx")
     core = lax.rem(ctx, 2)
@@ -87,6 +91,8 @@
     z = lax.rem(chip, n_z)
     partner = ctx + 1 - 2 * core
     first = core == 0
+    rank = z // 2
+    is_root = lax.rem(z, 2) == core
     has_before = chip > 0
     has_after = chip < n_chip - 1
     feeds = jnp.logical_and(core == 1, has_after)
@@ -119,6 +125,7 @@
         sent.append(copy)
 
     peers = [(ds, dc) for ds in range(sections) for dc in range(2) if ds or dc]
+    peers.sort(key=lambda p: abs(p[0] - sections // 2))
 
     loads = [
         pltpu.make_async_copy(src, dst, in_s.at[n])
@@ -182,7 +189,7 @@
     RT[1] = x_all[D - 8 :, D:]
     pl.semaphore_wait(barrier, greeted)
 
-    for ds, dc in reversed(peers):
+    for ds, dc in peers:
         back = ((sections - ds) % sections) * 2 + dc
         go(R.at[0], R.at[back], row_s.at[ds * 2 + dc], row_r.at[back], side(ds), partner if dc else ctx)
     go(SB, XB.at[core], one_s.at[0], one_r.at[0], sec, partner)
@@ -299,9 +306,26 @@
     t0, t1 = MAPS[0, 0], MAPS[1, 0]
     TS[z] = mm(t1, t0)
 
-    direct = [dz for dz in range(1, n_z) if dz != half or n_z == 2]
-    for dz in sorted(direct, key=lambda dz: (min(dz, n_z - dz) > 1, -min(dz, n_z - dz))):
-        go(TS.at[z], TS.at[z], ring_s.at[dz], ring_r.at[n_z - dz], sec, at_z(lax.rem(z + dz, n_z)))
+    def root_at(j):
+        return at_z(2 * j + core)
+
+    def map_send(dj):
+        j = lax.rem(rank + dj, roots)
+        return copy_to(TS.at[z], TS.at[z], ring_s.at[dj], ring_r.at[z], sec, root_at(j))
+
+    def part_send(dj):
+        j = lax.rem(rank + dj, roots)
+        return copy_to(VS.at[j], VR.at[z], vec_s.at[dj], vec_r.at[z], sec, root_at(j))
+
+    def all_roots(send, act):
+        for dj in range(1, roots):
+            act(send(dj))
+
+        @pl.when(jnp.logical_not(is_root))
+        def _():
+            act(send(0))
+
+    all_roots(map_send, lambda copy: copy.start())
 
     for b in range(2):
         q, d_out, sc = QK[0, blk[b], :], XB[b, 1], scores[b]
@@ -316,102 +340,93 @@
         MAPS[b, 2] = mm_tn(d_out, qeff)
     i_pair = mm_nt(MAPS[0, 1], t1) + MAPS[1, 1]
     s_pair = MAPS[0, 2] + mm(MAPS[1, 2], t0)
-    for zz in range(n_z):
-        VS[zz, 0:cols, :] = i_pair[zz * cols : (zz + 1) * cols]
-        VS[zz, cols : 2 * cols, :] = s_pair[zz * cols : (zz + 1) * cols]
-    VR[z] = VS[z]
-    for dz in range(1, n_z):
-        to = lax.rem(z + dz, n_z)
-        go(VS.at[to], VR.at[z], vec_s.at[dz], vec_r.at[n_z - dz], sec, at_z(to))
-    if n_z > 2:
-        low, high = pl.ds(0, D // 2), pl.ds(D // 2, D // 2)
-        left, right = lax.rem(z + n_z - 1, n_z), lax.rem(z + 1, n_z)
-        arrives(TS.at[left], ring_r.at[n_z - 1])
-        go(TS.at[left, low], TS.at[left, low], ring_s.at[0], ring_r.at[0], sec, at_z(lax.rem(z + half - 1, n_z)))
-        arrives(TS.at[right], ring_r.at[1])
-        go(TS.at[right, high], TS.at[right, high], ring_s.at[half], ring_r.at[half], sec,
-           at_z(lax.rem(z + n_z - half + 1, n_z)))
+    for j in range(roots):
+        VS[j, 0] = i_pair[j * cols : (j + 1) * cols]
+        VS[j, 1] = s_pair[j * cols : (j + 1) * cols]
+    all_roots(part_send, lambda copy: copy.start())
 
     for b in range(2):
         h = mm_tn(scores[b], XB[b, 1])
         zk = mm_tn(inverses[b], jnp.concatenate([h, kes[b]], axis=1))
         ZK[b, 0] = zk[:, :D]
         ZK[b, 1] = zk[:, D:]
-    for dz in direct:
-        if n_z == 2 or dz not in (1, n_z - 1):
-            arrives(TS.at[lax.rem(z + dz, n_z)], ring_r.at[dz])
-    for dz in range(1, n_z):
-        arrives(VR.at[lax.rem(z + dz, n_z)], vec_r.at[dz])
-    if n_z > 2:
-        far = lax.rem(z + half, n_z)
-        arrives(TS.at[far, low], ring_r.at[0])
-        arrives(TS.at[far, high], ring_r.at[half])
-
+    DM[:, 0:8, :] = jnp.zeros((3, 8, D), F32)
+    DM[:, 8 + 2 * D :, :] = jnp.zeros((3, 8, D), F32)
     eye = jnp.where(r == c, 1.0, 0.0).astype(F32)
-    zero_map = jnp.zeros((D, D), F32)
-    UP[0] = jnp.concatenate([jnp.zeros((cols, D), F32), eye], axis=0)
-    DN[n_z - 1] = jnp.concatenate([jnp.zeros((cols, D), F32), eye], axis=0)
-    up = jnp.concatenate([VR[0, 0:cols, :], jnp.transpose(TS[0])], axis=0)
-    down = jnp.concatenate([VR[n_z - 1, cols : 2 * cols, :], TS[n_z - 1]], axis=0)
-    for step in range(1, n_z):
-        zu, zd = step, n_z - 1 - step
-        UP[zu] = up
-        DN[zd] = down
-        up = mm_nt(up, TS[zu]) + jnp.concatenate([VR[zu, 0:cols, :], zero_map], axis=0)
-        down = mm(down, TS[zd]) + jnp.concatenate([VR[zd, cols : 2 * cols, :], zero_map], axis=0)
-    XY[y, 0] = up[:cols]
-    XY[y, 1] = down[:cols]
-    for dy in range(1, n_y):
-        go(XY.at[y], XY.at[y], ya_s.at[dy], ya_r.at[n_y - dy], sec, at_y(lax.rem(y + dy, n_y)))
-
-    def map_copy(yy, dy):
+    mine = pl.ds(pl.multiple_of(rank * cols, cols), cols)
+
+    def ends_send(dy):
+        return copy_to(XY.at[y], XY.at[y], ya_s.at[dy], ya_r.at[n_y - dy], sec, at_y(lax.rem(y + dy, n_y)))
+
+    def total_send(yy, dy):
         slot = PY.at[yy - 1]
         return copy_to(slot, slot, yb_s.at[dy], yb_r.at[yy], sec, at_y(lax.rem(y + dy, n_y)))
 
-    for yy in range(1, n_y - 1):
-        @pl.when(y == yy)
-        def _():
-            PY[yy - 1] = up[cols:]
-            for dy in range(1, n_y):
-                map_copy(yy, dy).start()
-
-    for zz in range(n_z):
-        XS[zz, 0] = UP[zz, 0:cols, :]
-        XS[zz, 1] = DN[zz, 0:cols, :]
-    mine = pl.ds(pl.multiple_of(z * cols, cols), cols)
-    XF[:, mine, :] = XS[z]
-    for dz in range(1, n_z):
+    def slice_send(dz):
         to = lax.rem(z + dz, n_z)
-        go(XS.at[to], XF.at[:, mine], xf_s.at[dz], xf_r.at[n_z - dz], sec, at_z(to))
-
-    for dy in range(1, n_y):
-        arrives(XY.at[lax.rem(y + dy, n_y)], ya_r.at[dy])
-    for yy in range(1, n_y - 1):
-        @pl.when(y != yy)
-        def _():
-            arrives(PY.at[yy - 1], yb_r.at[yy])
-    enter = jnp.where(y > 0, XY[0, 0], 0.0)
-    leave = jnp.where(y < n_y - 1, XY[n_y - 1, 1], 0.0)
-    for step in range(1, n_y - 1):
-        yu, yd = step, n_y - 1 - step
-        enter = jnp.where(y > yu, mm(enter, PY[yu - 1]) + XY[yu, 0], enter)
-        leave = jnp.where(y < yd, mm_nt(leave, PY[yd - 1]) + XY[yd, 1], leave)
-    SG[0] = enter
-    SG[1] = leave
-    SGF[:, mine, :] = SG[...]
-    for dz in range(1, n_z):
-        go(SG, SGF.at[:, mine], sg_s.at[dz], sg_r.at[n_z - dz], sec, at_z(lax.rem(z + dz, n_z)))
-    for dz in range(1, n_z):
-        theirs = pl.ds(pl.multiple_of(lax.rem(z + dz, n_z) * cols, cols), cols)
-        arrives(XF.at[:, theirs], xf_r.at[dz])
-        arrives(SGF.at[:, theirs], sg_r.at[dz])
-
-    starts = [XF[0] + mm(SGF[0], UP[z, cols:, :]), None]
-    ends = [None, XF[1] + mm(SGF[1], DN[z, cols:, :])]
+        return copy_to(SS.at[to], ST.at[:, mine], sg_s.at[dz], sg_r.at[rank], sec, at_z(to))
+
+    @pl.when(is_root)
+    def _():
+        VR[z] = VS[rank]
+        for dz in range(1, n_z):
+            zz = lax.rem(z + dz, n_z)
+            arrives(TS.at[zz], ring_r.at[zz])
+            arrives(VR.at[zz], vec_r.at[zz])
+        none = jnp.zeros((D, D), F32)
+        up = jnp.concatenate([VR[0, 0], jnp.transpose(TS[0])], axis=0)
+        down = jnp.concatenate([VR[n_z - 1, 1], TS[n_z - 1]], axis=0)
+        for step in range(1, n_z):
+            zu, zd = step, n_z - 1 - step
+            UP[zu] = up
+            DN[zd] = down
+            up = mm_nt(up, TS[zu]) + jnp.concatenate([VR[zu, 0], none], axis=0)
+            down = mm(down, TS[zd]) + jnp.concatenate([VR[zd, 1], none], axis=0)
+        XY[y, 0] = up[:cols]
+        XY[y, 1] = down[:cols]
+        for dy in range(1, n_y):
+            ends_send(dy).start()
+        for yy in range(1, n_y - 1):
+            @pl.when(y == yy)
+            def _():
+                PY[yy - 1] = up[cols:]
+                for dy in range(1, n_y):
+                    total_send(yy, dy).start()
+
+        for dy in range(1, n_y):
+            arrives(XY.at[lax.rem(y + dy, n_y)], ya_r.at[dy])
+        for yy in range(1, n_y - 1):
+            @pl.when(y != yy)
+            def _():
+                arrives(PY.at[yy - 1], yb_r.at[yy])
+        enter = jnp.where(y > 0, XY[0, 0], 0.0)
+        leave = jnp.where(y < n_y - 1, XY[n_y - 1, 1], 0.0)
+        for step in range(1, n_y - 1):
+            yu, yd = step, n_y - 1 - step
+            enter = jnp.where(y > yu, mm(enter, PY[yu - 1]) + XY[yu, 0], enter)
+            leave = jnp.where(y < yd, mm_nt(leave, PY[yd - 1]) + XY[yd, 1], leave)
+
+        for zz in range(n_z):
+            SS[zz, 0] = enter if zz == 0 else UP[zz, :cols, :] + mm(enter, UP[zz, cols:, :])
+            SS[zz, 1] = leave if zz == n_z - 1 else DN[zz, :cols, :] + mm(leave, DN[zz, cols:, :])
+        ST[:, mine, :] = SS[z]
+        for dz in range(1, n_z):
+            slice_send(dz).start()
+
+    for dj in range(roots):
+        j = lax.rem(rank + dj, roots)
+        theirs = ST.at[:, pl.ds(pl.multiple_of(j * cols, cols), cols)]
+        if dj:
+            arrives(theirs, sg_r.at[j])
+        else:
+            @pl.when(jnp.logical_not(is_root))
+            def _():
+                arrives(theirs, sg_r.at[j])
+
+    starts = [ST[0], None]
+    ends = [None, ST[1]]
     starts[1] = mm_nt(starts[0], t0) + MAPS[0, 1]
     ends[0] = mm(ends[1], t1) + MAPS[1, 2]
-    DM[:, 0:8, :] = jnp.zeros((3, 8, D), F32)
-    DM[:, 8 + 2 * D :, :] = jnp.zeros((3, 8, D), F32)
     for b in range(2):
         q, k = QK[0, blk[b], :], QK[1, blk[b], :]
         beta, d_out = XB[b, 3], XB[b, 1]
@@ -445,7 +460,7 @@
     TB[0] = row_sums(d_norm[8 : 8 + D] * XB[0, 0])
     TB[1] = row_sums(d_norm[8 + D :] * XB[1, 0])
 
-    for ds, dc in reversed(peers):
+    for ds, dc in peers:
         back = ((sections - ds) % sections) * 2 + dc
         go(TB.at[1 - core if dc else core], R2.at[back], row2_s.at[ds * 2 + dc], row2_r.at[back],
            side(ds), partner if dc else ctx)
@@ -514,17 +529,27 @@
         for copy in rim_back_copies():
             copy.wait_send()
 
-    for yy in range(1, n_y - 1):
-        @pl.when(y == yy)
-        def _():
-            for dy in range(1, n_y):
-                map_copy(yy, dy).wait_send()
+    all_roots(map_send, lambda copy: copy.wait_send())
+    all_roots(part_send, lambda copy: copy.wait_send())
+
+    @pl.when(is_root)
+    def _():
+        for dy in range(1, n_y):
+            ends_send(dy).wait_send()
+        for dz in range(1, n_z):
+            slice_send(dz).wait_send()
+        for yy in range(1, n_y - 1):
+            @pl.when(y == yy)
+            def _():
+                for dy in range(1, n_y):
+                    total_send(yy, dy).wait_send()
 
 
 def solution(mesh):
     sections, n_ctx = mesh.shape["section"], mesh.shape["ctx"]
     n_y, n_z = (4, 8) if n_ctx == 64 else (2, n_ctx // 4)
-    cols = D // n_z
+    roots = n_z // 2
+    cols = D // roots
     dma = lambda n: pltpu.SemaphoreType.DMA((n,))
 
     def shards(inputs, out_grads, conv_weight, log_decay, beta):
@@ -535,13 +560,13 @@
             v(4, D, D), v(2, 4, D, D), v(2 * sections, 8, D), v(2 * sections, 8, D), v(3, 8, D),
             v(2 * D + 8, D), v(sections, 8, D), v(8, D), v(2, D, D), v(3, 8, D), v(2 * sections, 8, D), v(2, 8, D),
             v(3, 2 * D, D), v(3, 2 * D, D), v(2, 4, D, D), v(2, 3 * D, D), v(2, 2 * D, D), v(2, 2, D, D),
-            v(2, 2, D, D), v(2, 3, D, D), v(n_z, D, D), v(n_z, 2 * cols, D), v(n_z, 2 * cols, D),
-            v(n_z, cols + D, D), v(n_z, cols + D, D), v(n_z, 2, cols, D), v(2, D, D), v(n_y, 2, cols, D),
-            v(max(n_y - 2, 1), D, D), v(2, cols, D), v(2, D, D), v(3, 2 * D + 16, D),
+            v(2, 2, D, D), v(2, 3, D, D), v(n_z, D, D), v(roots, 2, cols, D), v(n_z, 2, cols, D),
+            v(n_z, cols + D, D), v(n_z, cols + D, D), v(n_y, 2, cols, D),
+            v(max(n_y - 2, 1), D, D), v(n_z, 2, cols, D), v(2, D, D), v(3, 2 * D + 16, D),
             v(2, D, D), v(D, D), v(2, D, D), v(D, D),
             dma(5), dma(2 * sections), dma(2 * sections), dma(2 * sections + 2), dma(sections + 1),
             dma(2 * sections), dma(2 * sections), dma(sections + 1), dma(2 * sections + 2), dma(3), dma(3),
-            dma(n_z), dma(n_z), dma(n_z), dma(n_z), dma(n_z), dma(n_z), dma(n_z), dma(n_z),
+            dma(roots), dma(n_z), dma(roots), dma(n_z), dma(n_z), dma(roots),
             dma(n_y), dma(n_y), dma(n_y), dma(n_y),
         ]
         vm = pl.BlockSpec(memory_space=pltpu.VMEM)

time: 71.1 us -> 66.5 us (0.935)
  Pallas kernels: 68.1 us -> 63.6 us
    pallas_call x1, Pallas kernels: 68.1 us -> 63.6 us  [shards(): pl.pallas_call(functools.partial(kernel, (sections, n_y, n_z, width_all))...]
where the time goes in v3:
time: 66.5 us; the launch traced here: 66.4 us
  Pallas kernels  63.6 us (96%)
  local copies, waits for them, and re-layouts  2.14 us (3%)
    pallas_call x1, Pallas kernels, shards(): pl.pallas_call(functools.partial(kernel, (sections, n_y, n_z, width_all))...  63.6 us
    unnamed x4, local copies, waits for them, and re-layouts  2.14 us

profile of v3, /device:TPU:1, one launch (start us, length us, event | category | flops | bytes accessed | tf_op | source)
XLA Modules:
  0.0 66.4 jit_solution(13673516164199884955)
XLA Ops:
  0.6 63.6 %shard_map.68 = (bf16[128,256]{1,0:T(8,128)(2,1)}, bf16[128,256]{1,0:T(8,128)(2,1)}) custom-call(bf16[128,256]{1,0:T(8,128)(2,1)} %x_hbm.1, bf16[128,256]{1,0:T(8,128)(2,1)} %do_hbm.1, f32[128,256]{1,0:T(8,128)} %g_hbm.1, f32[2,128]{1,0:T(2,128)} %bitcast.1, f32[3,4,256]{2,1,0:T(4,128)} %w_hbm.1), custom_call_target="tpu_custom_call" | custom-call | tf_op jit(solution)/shard_map/pallas_call | solution.py:574
  64.2 0.0 copy-start
  64.2 1.5 %copy.9 = bf16[128,256]{1,0:T(8,128)(2,1)} copy(bf16[128,256]{1,0:T(8,128)(2,1)} %get-tuple-element.4) | data formatting | bytes 131072
  65.7 0.0 copy-done
  65.7 0.6 copy.10
Async XLA Ops:
  64.2 1.5 %copy-start = (bf16[128,256]{1,0:T(8,128)(2,1)S(1)}, bf16[128,256]{1,0:T(8,128)(2,1)}, u32[]{:S(2)}) copy-start(bf16[128,256]{1,0:T(8,128)(2,1)} %get-tuple-element.5) | copy-start | bytes 196612

commit v4 on v3

--- a/solution.py
+++ b/solution.py
@@ -75,7 +75,7 @@
     (
         x_ref, do_ref, g_ref, beta_ref, w_ref,
         SB, XB, R, R2, TB, NP, RIM, RIMR, SC, GRIM, RIM2, RT,
-        QK, DS, EX, FB, WQ, UO, ZK, MAPS, TS, VS, VR, UP, DN, XY, PY, SS, ST, DM, OB, OR, GB, GR,
+        QK, DS, EX, FB, WQ, UO, ZK, MAPS, TS, VS, VR, UP, DN, XY, PY, SS, ST, DM, OB, OR, GB, GR, FIN, RT2,
         in_s, row_s, row_r, rim_s, rim_r, row2_s, row2_r, rim2_s, rim2_r, one_s, one_r,
         ring_s, ring_r, vec_s, vec_r, sg_s, sg_r, ya_s, ya_r, yb_s, yb_r,
     ) = scratch
@@ -141,23 +141,23 @@
     def greet(to_sec, to_ctx):
         pl.semaphore_signal(barrier, inc=1, device_id=(to_sec, to_ctx), device_id_type=MESH)
 
+    @pl.when(has_before)
+    def _():
+        for ds in range(sections):
+            greet(side(ds), before_tail)
+
+    @pl.when(feeds)
+    def _():
+        for ds in range(sections):
+            for dc in range(2):
+                greet(side(ds), after_chip + dc)
+
     for ds, dc in peers:
         greet(side(ds), partner if dc else ctx)
     for dz in range(1, n_z):
         greet(sec, at_z(lax.rem(z + dz, n_z)))
     for dy in range(1, n_y):
         greet(sec, at_y(lax.rem(y + dy, n_y)))
-
-    @pl.when(has_before)
-    def _():
-        for ds in range(sections):
-            greet(side(ds), before_tail)
-
-    @pl.when(feeds)
-    def _():
-        for ds in range(sections):
-            for dc in range(2):
-                greet(side(ds), after_chip + dc)
 
     greeted = (
         len(peers) + n_z - 1 + n_y - 1
@@ -318,7 +318,7 @@
         return copy_to(VS.at[j], VR.at[z], vec_s.at[dj], vec_r.at[z], sec, root_at(j))
 
     def all_roots(send, act):
-        for dj in range(1, roots):
+        for dj in sorted(range(1, roots), key=lambda dj: abs(2 * dj - roots)):
             act(send(dj))
 
         @pl.when(jnp.logical_not(is_root))
@@ -374,6 +374,8 @@
             arrives(TS.at[zz], ring_r.at[zz])
             arrives(VR.at[zz], vec_r.at[zz])
         none = jnp.zeros((D, D), F32)
+        UP[0] = jnp.concatenate([jnp.zeros((cols, D), F32), eye], axis=0)
+        DN[n_z - 1] = UP[0]
         up = jnp.concatenate([VR[0, 0], jnp.transpose(TS[0])], axis=0)
         down = jnp.concatenate([VR[n_z - 1, 1], TS[n_z - 1]], axis=0)
         for step in range(1, n_z):
@@ -382,16 +384,16 @@
             DN[zd] = down
             up = mm_nt(up, TS[zu]) + jnp.concatenate([VR[zu, 0], none], axis=0)
             down = mm(down, TS[zd]) + jnp.concatenate([VR[zd, 1], none], axis=0)
-        XY[y, 0] = up[:cols]
-        XY[y, 1] = down[:cols]
-        for dy in range(1, n_y):
-            ends_send(dy).start()
         for yy in range(1, n_y - 1):
             @pl.when(y == yy)
             def _():
                 PY[yy - 1] = up[cols:]
-                for dy in range(1, n_y):
+                for dy in sorted(range(1, n_y), key=lambda dy: abs(2 * dy - n_y)):
                     total_send(yy, dy).start()
+        XY[y, 0] = up[:cols]
+        XY[y, 1] = down[:cols]
+        for dy in sorted(range(1, n_y), key=lambda dy: abs(2 * dy - n_y)):
+            ends_send(dy).start()
 
         for dy in range(1, n_y):
             arrives(XY.at[lax.rem(y + dy, n_y)], ya_r.at[dy])
@@ -406,12 +408,13 @@
             enter = jnp.where(y > yu, mm(enter, PY[yu - 1]) + XY[yu, 0], enter)
             leave = jnp.where(y < yd, mm_nt(leave, PY[yd - 1]) + XY[yd, 1], leave)
 
-        for zz in range(n_z):
-            SS[zz, 0] = enter if zz == 0 else UP[zz, :cols, :] + mm(enter, UP[zz, cols:, :])
-            SS[zz, 1] = leave if zz == n_z - 1 else DN[zz, :cols, :] + mm(leave, DN[zz, cols:, :])
+        for dz in sorted(range(n_z), key=lambda dz: (dz == 0, abs(2 * dz - n_z))):
+            zz = lax.rem(z + dz, n_z)
+            SS[zz, 0] = UP[zz, :cols, :] + mm(enter, UP[zz, cols:, :])
+            SS[zz, 1] = DN[zz, :cols, :] + mm(leave, DN[zz, cols:, :])
+            if dz:
+                slice_send(dz).start()
         ST[:, mine, :] = SS[z]
-        for dz in range(1, n_z):
-            slice_send(dz).start()
 
     for dj in range(roots):
         j = lax.rem(rank + dj, roots)
@@ -479,42 +482,40 @@
 
     go(GB.at[1 - core], GR, one_s.at[2], one_r.at[2], sec, partner)
 
+    def joined(own, oth):
+        return jnp.concatenate([jnp.where(first, own, oth), jnp.where(first, oth, own)], axis=1)
+
+    arrives(OR, one_r.at[1])
+    x_wide = x_ref[...].astype(F32)
+    out_ref[...] = (x_wide + joined(OB[core], OR[...])).astype(BF16)
+    arrives(GR, one_r.at[2])
+    scale = SC[core]
+    wide_scale = jnp.concatenate([scale, scale], axis=1)
+    FIN[...] = do_ref[...].astype(F32) + joined(GB[core], GR[...]) * wide_scale
+
+    for ds, dc in peers:
+        slot = ds * 2 + dc
+        arrives(R2.at[slot], row2_r.at[slot])
+    inner = TB[core]
+    for slot in range(1, 2 * sections):
+        inner = inner + R2[slot]
+    RT2[0] = inner
+
     @pl.when(feeds)
     def _():
         for slot in range(2 * sections):
             arrives(RIM2.at[slot], rim2_r.at[slot])
         for n in range(2):
             arrives(GRIM.at[n], rim2_r.at[2 * sections + n])
-
-    @pl.when(jnp.logical_not(feeds))
-    def _():
-        RIM2[...] = jnp.zeros((2 * sections, 8, D), F32)
-        GRIM[0] = jnp.zeros((8, D), F32)
-        GRIM[1] = jnp.zeros((8, D), F32)
-
-    for ds, dc in peers:
-        slot = ds * 2 + dc
-        arrives(R2.at[slot], row2_r.at[slot])
-    inner = TB[core] + RIM2[0]
-    for slot in range(1, 2 * sections):
-        inner = inner + R2[slot] + RIM2[slot]
-    scale = SC[core]
-    coef = as_columns(scale_same * scale_same * scale_same * inner / width_all)
-    arrives(OR, one_r.at[1])
-    arrives(GR, one_r.at[2])
-
-    def joined(own, oth):
-        return jnp.concatenate([jnp.where(first, own, oth), jnp.where(first, oth, own)], axis=1)
-
-    out_ref[...] = (x_ref[...].astype(F32) + joined(OB[core], OR[...])).astype(BF16)
-    late = jnp.concatenate([GRIM[0], GRIM[1]], axis=1)
-    grads = joined(GB[core], GR[...])
-    grads = jnp.concatenate([grads[: D - 8], grads[D - 8 :] + late], axis=0)
-    wide_scale = jnp.concatenate([scale, scale], axis=1)
-    wide_coef = jnp.concatenate([coef, coef], axis=1)
-    dx_ref[...] = (
-        do_ref[...].astype(F32) + grads * wide_scale - x_ref[...].astype(F32) * wide_coef
-    ).astype(BF16)
+        total = RT2[0]
+        for slot in range(2 * sections):
+            total = total + RIM2[slot]
+        RT2[0] = total
+        late = jnp.concatenate([GRIM[0], GRIM[1]], axis=1)
+        FIN[D - 8 :, :] = FIN[D - 8 :, :] + late * jnp.concatenate([SC[core, D - 8 :, :]] * 2, axis=1)
+
+    coef = as_columns(scale_same * scale_same * scale_same * RT2[0] / width_all)
+    dx_ref[...] = (FIN[...] - x_wide * jnp.concatenate([coef, coef], axis=1)).astype(BF16)
 
     for copy in sent:
         copy.wait_send()
@@ -563,7 +564,7 @@
             v(2, 2, D, D), v(2, 3, D, D), v(n_z, D, D), v(roots, 2, cols, D), v(n_z, 2, cols, D),
             v(n_z, cols + D, D), v(n_z, cols + D, D), v(n_y, 2, cols, D),
             v(max(n_y - 2, 1), D, D), v(n_z, 2, cols, D), v(2, D, D), v(3, 2 * D + 16, D),
-            v(2, D, D), v(D, D), v(2, D, D), v(D, D),
+            v(2, D, D), v(D, D), v(2, D, D), v(D, D), v(D, 2 * D), v(1, 8, D),
             dma(5), dma(2 * sections), dma(2 * sections), dma(2 * sections + 2), dma(sections + 1),
             dma(2 * sections), dma(2 * sections), dma(sections + 1), dma(2 * sections + 2), dma(3), dma(3),
             dma(roots), dma(n_z), dma(roots), dma(n_z), dma(n_z), dma(roots),
@@ -578,9 +579,9 @@
             out_specs=(vm, vm),
             scratch_shapes=scratch,
             compiler_params=pltpu.CompilerParams(
-                collective_id=0, has_side_effects=True, vmem_limit_bytes=64 * 2**20 - 2**18
+                collective_id=0, has_side_effects=True, vmem_limit_bytes=40 * 2**20
             ),
-        )(inputs, out_grads, log_decay, beta.T, conv_weight)
+        )(*[pltpu.with_memory_space_constraint(a, pltpu.MemorySpace.HBM) for a in (inputs, out_grads, log_decay, beta.T, conv_weight)])
 
     spec = P("ctx", "section")
     return jax.shard_map(

time: 66.5 us -> 62.6 us (0.941)
  Pallas kernels: 63.6 us -> 60.6 us
  local copies, waits for them, and re-layouts: 2.14 us -> 1.26 us
    pallas_call x1, Pallas kernels: 63.6 us -> 60.6 us  [shards(): pl.pallas_call(functools.partial(kernel, (sections, n_y, n_z, width_all))...]
    unnamed x4 -> x2, local copies, waits for them, and re-layouts: 2.14 us -> 1.26 us
where the time goes in v4:
time: 62.6 us; the launch traced here: 62.5 us
  Pallas kernels  60.6 us (97%)
  local copies, waits for them, and re-layouts  1.26 us (2%)
  between operations  0.64 us (1%)
    pallas_call x1, Pallas kernels, shards(): pl.pallas_call(functools.partial(kernel, (sections, n_y, n_z, width_all))...  60.6 us
    unnamed x2, local copies, waits for them, and re-layouts  1.26 us

profile of v4, /device:TPU:1, one launch (start us, length us, event | category | flops | bytes accessed | tf_op | source)
XLA Modules:
  0.0 62.5 jit_solution(9367552024716052142)
XLA Ops:
  0.6 60.6 %shard_map.68 = (bf16[128,256]{1,0:T(8,128)(2,1)S(1)}, bf16[128,256]{1,0:T(8,128)(2,1)S(1)}) custom-call(bf16[128,256]{1,0:T(8,128)(2,1)} %x_hbm.1, bf16[128,256]{1,0:T(8,128)(2,1)} %do_hbm.1, f32[128,256]{1,0:T(8,128)} %g_hbm.1, f32[2,128]{1,0:T(2,128)} %bitcast.1, f32[3,4,256]{2,1,0:T(4,128)} %w_hbm.1), custom_call_target="tpu_custom_call" | custom-call | tf_op jit(solution)/shard_map/pallas_call | solution.py:575
  61.2 0.6 %copy.9 = bf16[128,256]{1,0:T(8,128)(2,1)} copy(bf16[128,256]{1,0:T(8,128)(2,1)S(1)} %get-tuple-element.4) | data formatting | bytes 131072
  61.9 0.6 %copy.10 = bf16[128,256]{1,0:T(8,128)(2,1)} copy(bf16[128,256]{1,0:T(8,128)(2,1)S(1)} %get-tuple-element.5) | data formatting | bytes 131072

commit v5 on v4

--- a/solution.py
+++ b/solution.py
@@ -66,8 +66,9 @@
             inverse = [eye - o for o in off]
         else:
             half = [mm(m, o) for m, o in zip(inverse, off)]
+            if k == 6:
+                return inverse, half
             inverse = [m - mm(h, m) for h, m in zip(half, inverse)]
-    return inverse
 
 
 def kernel(geom, x_hbm, do_hbm, g_hbm, beta_hbm, w_hbm, out_ref, dx_ref, *scratch):
@@ -127,6 +128,34 @@
     peers = [(ds, dc) for ds in range(sections) for dc in range(2) if ds or dc]
     peers.sort(key=lambda p: abs(p[0] - sections // 2))
 
+    barrier = pltpu.get_barrier_semaphore()
+
+    def greet(to_sec, to_ctx):
+        pl.semaphore_signal(barrier, inc=1, device_id=(to_sec, to_ctx), device_id_type=MESH)
+
+    @pl.when(has_before)
+    def _():
+        for ds in range(sections):
+            greet(side(ds), before_tail)
+
+    @pl.when(feeds)
+    def _():
+        for ds in range(sections):
+            for dc in range(2):
+                greet(side(ds), after_chip + dc)
+
+    for ds, dc in peers:
+        greet(side(ds), partner if dc else ctx)
+    for dz in range(1, n_z):
+        greet(sec, at_z(lax.rem(z + dz, n_z)))
+    for dy in range(1, n_y):
+        greet(sec, at_y(lax.rem(y + dy, n_y)))
+
+    greeted = (
+        len(peers) + n_z - 1 + n_y - 1
+        + sections * has_before.astype(jnp.int32) + 2 * sections * feeds.astype(jnp.int32)
+    )
+
     loads = [
         pltpu.make_async_copy(src, dst, in_s.at[n])
         for n, (src, dst) in enumerate(
@@ -136,34 +165,6 @@
     for load in loads:
         load.start()
 
-    barrier = pltpu.get_barrier_semaphore()
-
-    def greet(to_sec, to_ctx):
-        pl.semaphore_signal(barrier, inc=1, device_id=(to_sec, to_ctx), device_id_type=MESH)
-
-    @pl.when(has_before)
-    def _():
-        for ds in range(sections):
-            greet(side(ds), before_tail)
-
-    @pl.when(feeds)
-    def _():
-        for ds in range(sections):
-            for dc in range(2):
-                greet(side(ds), after_chip + dc)
-
-    for ds, dc in peers:
-        greet(side(ds), partner if dc else ctx)
-    for dz in range(1, n_z):
-        greet(sec, at_z(lax.rem(z + dz, n_z)))
-    for dy in range(1, n_y):
-        greet(sec, at_y(lax.rem(y + dy, n_y)))
-
-    greeted = (
-        len(peers) + n_z - 1 + n_y - 1
-        + sections * has_before.astype(jnp.int32) + 2 * sections * feeds.astype(jnp.int32)
-    )
-
     for load in loads:
         load.wait()
 
@@ -173,7 +174,7 @@
         return jnp.where(first, low, high), jnp.where(first, high, low), whole
 
     x_own, x_oth, x_all = halves(x_ref)
-    R[0] = row_sums(x_all * x_all)
+    R[0] = row_sums(x_all * x_all)[0:1]
     d_own, d_oth, _ = halves(do_ref)
     g_own, g_oth, _ = halves(g_ref)
     b0, b1 = as_columns(beta_ref[0:1, :]), as_columns(beta_ref[1:2, :])
@@ -294,12 +295,13 @@
         both = mm_nt(jnp.concatenate([kf, qf], axis=0), kb)
         systems.append(jnp.where(strict, XB[b, 3] * both[:D], 0.0))
         scores.append(jnp.where(incl, both[D:], 0.0))
-    inverses = unit_lower_inverse(systems)
+    inverses, halved = unit_lower_inverse(systems)
     wus, kes = [], []
     for b in range(2):
         k, v, beta = QK[1, blk[b], :], QK[2, blk[b], :], XB[b, 3]
         ke = k * EX[b, 3]
         wu = mm(inverses[b], jnp.concatenate([beta * k * EX[b, 2], beta * v], axis=1))
+        wu = wu - mm(halved[b], wu)
         MAPS[b, 0] = jnp.where(r == c, jnp.exp(fins[b]), 0.0) - mm_tn(ke, wu[:, :D])
         wus.append(wu)
         kes.append(ke)
@@ -347,9 +349,17 @@
 
     for b in range(2):
         h = mm_tn(scores[b], XB[b, 1])
-        zk = mm_tn(inverses[b], jnp.concatenate([h, kes[b]], axis=1))
+        zk = mm_tn(inverses[b] - mm(halved[b], inverses[b]), jnp.concatenate([h, kes[b]], axis=1))
         ZK[b, 0] = zk[:, :D]
         ZK[b, 1] = zk[:, D:]
+    WS = WQ[1]
+    by_start = mm_nt(WS, MAPS[0, 1])
+    UO[1, 0] = UO[1, 0] - by_start[:D]
+    UO[1, 1] = UO[1, 1] + by_start[D:]
+    WQ[1] = mm(WS, t0)
+    KS = ZK[0, 1]
+    ZK[0, 0] = ZK[0, 0] + mm_nt(KS, MAPS[1, 2])
+    ZK[0, 1] = mm_nt(KS, t1)
     DM[:, 0:8, :] = jnp.zeros((3, 8, D), F32)
     DM[:, 8 + 2 * D :, :] = jnp.zeros((3, 8, D), F32)
     eye = jnp.where(r == c, 1.0, 0.0).astype(F32)
@@ -433,10 +443,10 @@
     for b in range(2):
         q, k = QK[0, blk[b], :], QK[1, blk[b], :]
         beta, d_out = XB[b, 3], XB[b, 1]
-        wq = mm_nt(WQ[b], starts[b])
+        wq = mm_nt(WQ[b], starts[0])
         fresh = UO[b, 0] - wq[:D]
         OB[b] = UO[b, 1] + wq[D:]
-        zeta = ZK[b, 0] + mm_nt(ZK[b, 1], ends[b])
+        zeta = ZK[b, 0] + mm_nt(ZK[b, 1], ends[1])
         pair = mm_nt(jnp.concatenate([d_out, zeta], axis=0), fresh)
         d_sc = jnp.where(incl, pair[:D], 0.0)
         d_p = beta * jnp.where(strict, -pair[D:], 0.0)
@@ -459,9 +469,9 @@
     GB[0] = d_norm[8 : 8 + D]
     GB[1] = d_norm[8 + D :]
     GRIM[2] = d_norm[:8]
-    TB[2] = row_sums(jnp.concatenate([jnp.zeros((D - 8, D), F32), d_norm[:8] * RIMR[...]], axis=0))
-    TB[0] = row_sums(d_norm[8 : 8 + D] * XB[0, 0])
-    TB[1] = row_sums(d_norm[8 + D :] * XB[1, 0])
+    TB[2] = row_sums(jnp.concatenate([jnp.zeros((D - 8, D), F32), d_norm[:8] * RIMR[...]], axis=0))[0:1]
+    TB[0] = row_sums(d_norm[8 : 8 + D] * XB[0, 0])[0:1]
+    TB[1] = row_sums(d_norm[8 + D :] * XB[1, 0])[0:1]
 
     for ds, dc in peers:
         back = ((sections - ds) % sections) * 2 + dc
@@ -558,13 +568,13 @@
         v = lambda *s: pltpu.VMEM(s, F32)
         scratch = [
             pltpu.VMEM((D, 2 * D), BF16), pltpu.VMEM((D, 2 * D), BF16), v(D, 2 * D), v(2, D), v(3, 4, 2 * D),
-            v(4, D, D), v(2, 4, D, D), v(2 * sections, 8, D), v(2 * sections, 8, D), v(3, 8, D),
-            v(2 * D + 8, D), v(sections, 8, D), v(8, D), v(2, D, D), v(3, 8, D), v(2 * sections, 8, D), v(2, 8, D),
+            v(4, D, D), v(2, 4, D, D), v(2 * sections, 1, D), v(2 * sections, 1, D), v(3, 1, D),
+            v(2 * D + 8, D), v(sections, 1, D), v(8, D), v(2, D, D), v(3, 8, D), v(2 * sections, 1, D), v(2, 8, D),
             v(3, 2 * D, D), v(3, 2 * D, D), v(2, 4, D, D), v(2, 3 * D, D), v(2, 2 * D, D), v(2, 2, D, D),
             v(2, 2, D, D), v(2, 3, D, D), v(n_z, D, D), v(roots, 2, cols, D), v(n_z, 2, cols, D),
             v(n_z, cols + D, D), v(n_z, cols + D, D), v(n_y, 2, cols, D),
             v(max(n_y - 2, 1), D, D), v(n_z, 2, cols, D), v(2, D, D), v(3, 2 * D + 16, D),
-            v(2, D, D), v(D, D), v(2, D, D), v(D, D), v(D, 2 * D), v(1, 8, D),
+            v(2, D, D), v(D, D), v(2, D, D), v(D, D), v(D, 2 * D), v(1, 1, D),
             dma(5), dma(2 * sections), dma(2 * sections), dma(2 * sections + 2), dma(sections + 1),
             dma(2 * sections), dma(2 * sections), dma(sections + 1), dma(2 * sections + 2), dma(3), dma(3),
             dma(roots), dma(n_z), dma(roots), dma(n_z), dma(n_z), dma(roots),

time: 62.6 us -> 60.3 us (0.963)
  Pallas kernels: 60.6 us -> 58.2 us
    pallas_call x1, Pallas kernels: 60.6 us -> 58.2 us  [shards(): pl.pallas_call(functools.partial(kernel, (sections, n_y, n_z, width_all))...]
where the time goes in v5:
time: 60.3 us; the launch traced here: 60.1 us
  Pallas kernels  58.2 us (97%)
  local copies, waits for them, and re-layouts  1.26 us (2%)
  between operations  0.64 us (1%)
    pallas_call x1, Pallas kernels, shards(): pl.pallas_call(functools.partial(kernel, (sections, n_y, n_z, width_all))...  58.2 us
    unnamed x2, local copies, waits for them, and re-layouts  1.26 us

profile of v5, /device:TPU:1, one launch (start us, length us, event | category | flops | bytes accessed | tf_op | source)
XLA Modules:
  0.0 60.1 jit_solution(4966188952270097542)
XLA Ops:
  0.6 58.2 %shard_map.68 = (bf16[128,256]{1,0:T(8,128)(2,1)S(1)}, bf16[128,256]{1,0:T(8,128)(2,1)S(1)}) custom-call(bf16[128,256]{1,0:T(8,128)(2,1)} %x_hbm.1, bf16[128,256]{1,0:T(8,128)(2,1)} %do_hbm.1, f32[128,256]{1,0:T(8,128)} %g_hbm.1, f32[2,128]{1,0:T(2,128)} %bitcast.1, f32[3,4,256]{2,1,0:T(4,128)} %w_hbm.1), custom_call_target="tpu_custom_call" | custom-call | tf_op jit(solution)/shard_map/pallas_call | solution.py:585
  58.9 0.6 %copy.9 = bf16[128,256]{1,0:T(8,128)(2,1)} copy(bf16[128,256]{1,0:T(8,128)(2,1)S(1)} %get-tuple-element.4) | data formatting | bytes 131072
  59.5 0.6 %copy.10 = bf16[128,256]{1,0:T(8,128)(2,1)} copy(bf16[128,256]{1,0:T(8,128)(2,1)S(1)} %get-tuple-element.5) | data formatting | bytes 131072

commit v6 on v5

--- a/solution.py
+++ b/solution.py
@@ -76,7 +76,7 @@
     (
         x_ref, do_ref, g_ref, beta_ref, w_ref,
         SB, XB, R, R2, TB, NP, RIM, RIMR, SC, GRIM, RIM2, RT,
-        QK, DS, EX, FB, WQ, UO, ZK, MAPS, TS, VS, VR, UP, DN, XY, PY, SS, ST, DM, OB, OR, GB, GR, FIN, RT2,
+        QK, DS, EX, FB, WQ, UO, ZK, MAPS, TS, VS, VR, PU, PD, XU, XD, XY, PY, SS, ST, DM, OB, OR, GB, GR, FIN, RT2,
         in_s, row_s, row_r, rim_s, rim_r, row2_s, row2_r, rim2_s, rim2_r, one_s, one_r,
         ring_s, ring_r, vec_s, vec_r, sg_s, sg_r, ya_s, ya_r, yb_s, yb_r,
     ) = scratch
@@ -382,28 +382,45 @@
         for dz in range(1, n_z):
             zz = lax.rem(z + dz, n_z)
             arrives(TS.at[zz], ring_r.at[zz])
-            arrives(VR.at[zz], vec_r.at[zz])
-        none = jnp.zeros((D, D), F32)
-        UP[0] = jnp.concatenate([jnp.zeros((cols, D), F32), eye], axis=0)
-        DN[n_z - 1] = UP[0]
-        up = jnp.concatenate([VR[0, 0], jnp.transpose(TS[0])], axis=0)
-        down = jnp.concatenate([VR[n_z - 1, 1], TS[n_z - 1]], axis=0)
+        PU[0] = eye
+        PD[n_z - 1] = eye
+        up, down = jnp.transpose(TS[0]), TS[n_z - 1]
         for step in range(1, n_z):
             zu, zd = step, n_z - 1 - step
-            UP[zu] = up
-            DN[zd] = down
-            up = mm_nt(up, TS[zu]) + jnp.concatenate([VR[zu, 0], none], axis=0)
-            down = mm(down, TS[zd]) + jnp.concatenate([VR[zd, 1], none], axis=0)
+            PU[zu] = up
+            PD[zd] = down
+            up = mm_nt(up, TS[zu])
+            down = mm(down, TS[zd])
         for yy in range(1, n_y - 1):
             @pl.when(y == yy)
             def _():
-                PY[yy - 1] = up[cols:]
+                PY[yy - 1] = up
                 for dy in sorted(range(1, n_y), key=lambda dy: abs(2 * dy - n_y)):
                     total_send(yy, dy).start()
-        XY[y, 0] = up[:cols]
-        XY[y, 1] = down[:cols]
+
+        for dz in range(1, n_z):
+            zz = lax.rem(z + dz, n_z)
+            arrives(VR.at[zz], vec_r.at[zz])
+        all_up, all_down = VR[n_z - 1, 0], VR[0, 1]
+        for step in range(1, n_z):
+            zu, zd = n_z - 1 - step, step
+            all_up = all_up + mm_nt(VR[zu, 0], PD[zu])
+            all_down = all_down + mm_nt(VR[zd, 1], PU[zd])
+        XY[y, 0] = all_up
+        XY[y, 1] = all_down
         for dy in sorted(range(1, n_y), key=lambda dy: abs(2 * dy - n_y)):
             ends_send(dy).start()
+
+        up, down = VR[0, 0], VR[n_z - 1, 1]
+        XU[0] = jnp.zeros((cols, D), F32)
+        XD[n_z - 1] = jnp.zeros((cols, D), F32)
+        for step in range(1, n_z):
+            zu, zd = step, n_z - 1 - step
+            XU[zu] = up
+            XD[zd] = down
+            if step < n_z - 1:
+                up = mm_nt(up, TS[zu]) + VR[zu, 0]
+                down = mm(down, TS[zd]) + VR[zd, 1]
 
         for dy in range(1, n_y):
             arrives(XY.at[lax.rem(y + dy, n_y)], ya_r.at[dy])
@@ -420,8 +437,8 @@
 
         for dz in sorted(range(n_z), key=lambda dz: (dz == 0, abs(2 * dz - n_z))):
             zz = lax.rem(z + dz, n_z)
-            SS[zz, 0] = UP[zz, :cols, :] + mm(enter, UP[zz, cols:, :])
-            SS[zz, 1] = DN[zz, :cols, :] + mm(leave, DN[zz, cols:, :])
+            SS[zz, 0] = XU[zz] + mm(enter, PU[zz])
+            SS[zz, 1] = XD[zz] + mm(leave, PD[zz])
             if dz:
                 slice_send(dz).start()
         ST[:, mine, :] = SS[z]
@@ -572,7 +589,7 @@
             v(2 * D + 8, D), v(sections, 1, D), v(8, D), v(2, D, D), v(3, 8, D), v(2 * sections, 1, D), v(2, 8, D),
             v(3, 2 * D, D), v(3, 2 * D, D), v(2, 4, D, D), v(2, 3 * D, D), v(2, 2 * D, D), v(2, 2, D, D),
             v(2, 2, D, D), v(2, 3, D, D), v(n_z, D, D), v(roots, 2, cols, D), v(n_z, 2, cols, D),
-            v(n_z, cols + D, D), v(n_z, cols + D, D), v(n_y, 2, cols, D),
+            v(n_z, D, D), v(n_z, D, D), v(n_z, cols, D), v(n_z, cols, D), v(n_y, 2, cols, D),
             v(max(n_y - 2, 1), D, D), v(n_z, 2, cols, D), v(2, D, D), v(3, 2 * D + 16, D),
             v(2, D, D), v(D, D), v(2, D, D), v(D, D), v(D, 2 * D), v(1, 1, D),
             dma(5), dma(2 * sections), dma(2 * sections), dma(2 * sections + 2), dma(sections + 1),

time: 60.3 us -> 58.9 us (0.977)
  Pallas kernels: 58.2 us -> 56.8 us
    pallas_call x1, Pallas kernels: 58.2 us -> 56.8 us  [shards(): pl.pallas_call(functools.partial(kernel, (sections, n_y, n_z, width_all))...]
where the time goes in v6:
time: 58.9 us; the launch traced here: 58.7 us
  Pallas kernels  56.8 us (96%)
  local copies, waits for them, and re-layouts  1.26 us (2%)
  between operations  0.64 us (1%)
    pallas_call x1, Pallas kernels, shards(): pl.pallas_call(functools.partial(kernel, (sections, n_y, n_z, width_all))...  56.8 us
    unnamed x2, local copies, waits for them, and re-layouts  1.26 us

profile of v6, /device:TPU:1, one launch (start us, length us, event | category | flops | bytes accessed | tf_op | source)
XLA Modules:
  0.0 58.7 jit_solution(6510247349029327253)
XLA Ops:
  0.6 56.8 %shard_map.68 = (bf16[128,256]{1,0:T(8,128)(2,1)S(1)}, bf16[128,256]{1,0:T(8,128)(2,1)S(1)}) custom-call(bf16[128,256]{1,0:T(8,128)(2,1)} %x_hbm.1, bf16[128,256]{1,0:T(8,128)(2,1)} %do_hbm.1, f32[128,256]{1,0:T(8,128)} %g_hbm.1, f32[2,128]{1,0:T(2,128)} %bitcast.1, f32[3,4,256]{2,1,0:T(4,128)} %w_hbm.1), custom_call_target="tpu_custom_call" | custom-call | tf_op jit(solution)/shard_map/pallas_call | solution.py:602
  57.5 0.6 %copy.9 = bf16[128,256]{1,0:T(8,128)(2,1)} copy(bf16[128,256]{1,0:T(8,128)(2,1)S(1)} %get-tuple-element.4) | data formatting | bytes 131072
  58.1 0.6 %copy.10 = bf16[128,256]{1,0:T(8,128)(2,1)} copy(bf16[128,256]{1,0:T(8,128)(2,1)S(1)} %get-tuple-element.5) | data formatting | bytes 131072

commit v7 on v6

--- a/solution.py
+++ b/solution.py
@@ -71,7 +71,7 @@
             inverse = [m - mm(h, m) for h, m in zip(half, inverse)]
 
 
-def kernel(geom, x_hbm, do_hbm, g_hbm, beta_hbm, w_hbm, out_ref, dx_ref, *scratch):
+def kernel(geom, x_hbm, do_hbm, g_hbm, beta_hbm, w_hbm, both_ref, *scratch):
     sections, n_y, n_z, width_all = geom
     (
         x_ref, do_ref, g_ref, beta_ref, w_ref,
@@ -514,7 +514,7 @@
 
     arrives(OR, one_r.at[1])
     x_wide = x_ref[...].astype(F32)
-    out_ref[...] = (x_wide + joined(OB[core], OR[...])).astype(BF16)
+    both_ref[0] = (x_wide + joined(OB[core], OR[...])).astype(BF16)
     arrives(GR, one_r.at[2])
     scale = SC[core]
     wide_scale = jnp.concatenate([scale, scale], axis=1)
@@ -542,7 +542,7 @@
         FIN[D - 8 :, :] = FIN[D - 8 :, :] + late * jnp.concatenate([SC[core, D - 8 :, :]] * 2, axis=1)
 
     coef = as_columns(scale_same * scale_same * scale_same * RT2[0] / width_all)
-    dx_ref[...] = (FIN[...] - x_wide * jnp.concatenate([coef, coef], axis=1)).astype(BF16)
+    both_ref[1] = (FIN[...] - x_wide * jnp.concatenate([coef, coef], axis=1)).astype(BF16)
 
     for copy in sent:
         copy.wait_send()
@@ -599,16 +599,17 @@
         ]
         vm = pl.BlockSpec(memory_space=pltpu.VMEM)
         hbm = pl.BlockSpec(memory_space=pltpu.MemorySpace.HBM)
-        return pl.pallas_call(
+        both = pl.pallas_call(
             functools.partial(kernel, (sections, n_y, n_z, width_all)),
-            out_shape=(jax.ShapeDtypeStruct(inputs.shape, BF16), jax.ShapeDtypeStruct(inputs.shape, BF16)),
+            out_shape=jax.ShapeDtypeStruct((2,) + inputs.shape, BF16),
             in_specs=[hbm] * 5,
-            out_specs=(vm, vm),
+            out_specs=vm,
             scratch_shapes=scratch,
             compiler_params=pltpu.CompilerParams(
                 collective_id=0, has_side_effects=True, vmem_limit_bytes=40 * 2**20
             ),
         )(*[pltpu.with_memory_space_constraint(a, pltpu.MemorySpace.HBM) for a in (inputs, out_grads, log_decay, beta.T, conv_weight)])
+        return both[0], both[1]
 
     spec = P("ctx", "section")
     return jax.shard_map(

time: 58.9 us -> 58.3 us (0.990)
  local copies, waits for them, and re-layouts: 1.26 us -> 0.66 us
    unnamed x2 -> x0, local copies, waits for them, and re-layouts: 1.26 us -> none
    squeeze x0 -> x1, local copies, waits for them, and re-layouts: none -> 0.66 us  [shards(): return (both[0], both[1])]
where the time goes in v7:
time: 58.3 us; the launch traced here: 58.1 us
  Pallas kernels  56.8 us (97%)
  local copies, waits for them, and re-layouts  0.66 us (1%)
  between operations  0.64 us (1%)
    pallas_call x1, Pallas kernels, shards(): pl.pallas_call(functools.partial(kernel, (sections, n_y, n_z, width_all))...  56.8 us

profile of v7, /device:TPU:1, one launch (start us, length us, event | category | flops | bytes accessed | tf_op | source)
XLA Modules:
  0.0 58.1 jit_solution(17106695195798016496)
XLA Ops:
  0.6 56.8 %shard_map.68 = bf16[2,128,256]{2,1,0:T(8,128)(2,1)S(1)} custom-call(bf16[128,256]{1,0:T(8,128)(2,1)} %x_hbm.1, bf16[128,256]{1,0:T(8,128)(2,1)} %do_hbm.1, f32[128,256]{1,0:T(8,128)} %g_hbm.1, f32[2,128]{1,0:T(2,128)} %bitcast.5, f32[3,4,256]{2,1,0:T(4,128)} %w_hbm.1), custom_call_target="tpu_custom_call" | custom-call | tf_op jit(solution)/shard_map/pallas_call | solution.py:602
  57.5 0.7 %slice_bitcast_fusion = (bf16[128,256]{1,0:T(8,128)(2,1)}, bf16[128,256]{1,0:T(8,128)(2,1)}) fusion(bf16[2,128,256]{2,1,0:T(8,128)(2,1)S(1)} %shard_map.68), kind=kLoop, calls=%fused_computation | loop fusion | bytes 262144 | tf_op jit(solution)/shard_map/squeeze | solution.py:612

commit v8 on v7

--- a/solution.py
+++ b/solution.py
@@ -190,11 +190,6 @@
     RT[1] = x_all[D - 8 :, D:]
     pl.semaphore_wait(barrier, greeted)
 
-    for ds, dc in peers:
-        back = ((sections - ds) % sections) * 2 + dc
-        go(R.at[0], R.at[back], row_s.at[ds * 2 + dc], row_r.at[back], side(ds), partner if dc else ctx)
-    go(SB, XB.at[core], one_s.at[0], one_r.at[0], sec, partner)
-
     def rim_copies():
         made = []
         for dc in range(2):
@@ -208,6 +203,11 @@
     def _():
         for copy in rim_copies():
             copy.start()
+
+    for ds, dc in peers:
+        back = ((sections - ds) % sections) * 2 + dc
+        go(R.at[0], R.at[back], row_s.at[ds * 2 + dc], row_r.at[back], side(ds), partner if dc else ctx)
+    go(SB, XB.at[core], one_s.at[0], one_r.at[0], sec, partner)
 
     arrives(XB.at[1 - core], one_r.at[0])
     r, c = iota2((D, D), 0), iota2((D, D), 1)
@@ -490,10 +490,7 @@
     TB[0] = row_sums(d_norm[8 : 8 + D] * XB[0, 0])[0:1]
     TB[1] = row_sums(d_norm[8 + D :] * XB[1, 0])[0:1]
 
-    for ds, dc in peers:
-        back = ((sections - ds) % sections) * 2 + dc
-        go(TB.at[1 - core if dc else core], R2.at[back], row2_s.at[ds * 2 + dc], row2_r.at[back],
-           side(ds), partner if dc else ctx)
+    go(GB.at[1 - core], GR, one_s.at[2], one_r.at[2], sec, partner)
 
     def rim_back_copies():
         made = [copy_to(GRIM.at[2], GRIM.at[core], rim2_s.at[sections], rim2_r.at[2 * sections + core], sec, before_tail)]
@@ -507,7 +504,11 @@
         for copy in rim_back_copies():
             copy.start()
 
-    go(GB.at[1 - core], GR, one_s.at[2], one_r.at[2], sec, partner)
+    for ds, dc in peers:
+        back = ((sections - ds) % sections) * 2 + dc
+        go(TB.at[1 - core if dc else core], R2.at[back], row2_s.at[ds * 2 + dc], row2_r.at[back],
+           side(ds), partner if dc else ctx)
+
 
     def joined(own, oth):
         return jnp.concatenate([jnp.where(first, own, oth), jnp.where(first, oth, own)], axis=1)

time: 58.3 us -> 58.3 us (level)
  no operation moved by 1% of the time
where the time goes in v8:
time: 58.3 us; the launch traced here: 58.1 us
  Pallas kernels  56.8 us (97%)
  local copies, waits for them, and re-layouts  0.66 us (1%)
  between operations  0.64 us (1%)
    pallas_call x1, Pallas kernels, shards(): pl.pallas_call(functools.partial(kernel, (sections, n_y, n_z, width_all))...  56.8 us

profile of v8, /device:TPU:1, one launch (start us, length us, event | category | flops | bytes accessed | tf_op | source)
XLA Modules:
  0.0 58.1 jit_solution(12960670649032695685)
XLA Ops:
  0.6 56.8 %shard_map.68 = bf16[2,128,256]{2,1,0:T(8,128)(2,1)S(1)} custom-call(bf16[128,256]{1,0:T(8,128)(2,1)} %x_hbm.1, bf16[128,256]{1,0:T(8,128)(2,1)} %do_hbm.1, f32[128,256]{1,0:T(8,128)} %g_hbm.1, f32[2,128]{1,0:T(2,128)} %bitcast.5, f32[3,4,256]{2,1,0:T(4,128)} %w_hbm.1), custom_call_target="tpu_custom_call" | custom-call | tf_op jit(solution)/shard_map/pallas_call | solution.py:603
  57.5 0.7 %slice_bitcast_fusion = (bf16[128,256]{1,0:T(8,128)(2,1)}, bf16[128,256]{1,0:T(8,128)(2,1)}) fusion(bf16[2,128,256]{2,1,0:T(8,128)(2,1)S(1)} %shard_map.68), kind=kLoop, calls=%fused_computation | loop fusion | bytes 262144 | tf_op jit(solution)/shard_map/squeeze | solution.py:613
